TPU v7x, 512 devices: a whole 4x4x16 slice. The times are simulated.
512 devices in a mesh: section: 32 (over z_hi, x, core), dp: 16 (over y, z_lo).
Axes of the slice: x: 4, y: 4, z: 16 (z_hi: 4, z_lo: 4; z = z_hi * 4 + z_lo), core: 2. Of those that a mesh axis runs over, the one named last changes fastest.
Arguments:
- saved_x: bfloat16 [2, 3, 32, 16, 16, 16, 128], P(None, None, 'section', 'dp'), may hold values from -6 to 6
- saved_h: bfloat16 [2, 3, 32, 16, 16, 16, 128], P(None, None, 'section', 'dp'), may hold values from -6 to 6
- kernels: bfloat16 [32, 2, 2, 9, 128, 128], P('section'), as said below
- grad_in: bfloat16 [2, 32, 16, 16, 16, 128], P(None, 'section', 'dp'), may hold values from -6 to 6
- loss_grads: bfloat16 [2, 2, 16, 16, 16, 128], P(None, None, 'dp'), may hold values from -6 to 6
Outputs:
- kernel_grads: float32 [32, 2304, 128], P('section', 'dp')
- edge_grads: bfloat16 [2, 32, 16, 16, 16, 128], P(None, 'section', 'dp')
Inputs may be any that keep to these rules, and one draw needn't show every extreme that they name: kernels[d, 1] equals kernels[31 - d, 0]: each position holds replica 1's copy of the mirrored section. Every entry lies within 3 / sqrt(1152) in magnitude.
All inputs are finite; a program needn't handle non-finite values.
Results may differ from a plain program's by a relative error of at most 0.0052.
Values may be sent and summed in bfloat16 or wider, within the bound.
No kernel may reach another device: no remote copies, remote signals or barrier semaphores. Data moves between devices by JAX's collectives and lax.ppermute only.
A program may use at most 64 MiB of HBM per device.

v0:
```python
import jax
import jax.numpy as jnp
from jax import lax
from jax.sharding import PartitionSpec as P


def from_behind(value, axis, by):
    peers = lax.axis_size(axis)
    pairs = [(i, i + by) for i in range(peers) if 0 <= i + by < peers]
    return lax.ppermute(value, axis, pairs)


def from_partner(value, axis, bit):
    mask = 2**bit
    pairs = [(source, source ^ mask) for source in range(lax.axis_size(axis))]
    return lax.ppermute(value, axis, pairs)


def tap_views(feature, sign):
    extent = feature.shape[1]
    padded = jnp.pad(feature, ((0, 0), (1, 1), (1, 1), (0, 0)))
    pieces = []
    for row_shift in (-1, 0, 1):
        for col_shift in (-1, 0, 1):
            row_start = 1 + sign * row_shift
            col_start = 1 + sign * col_shift
            pieces.append(
                padded[:, row_start : row_start + extent, col_start : col_start + extent, :]
            )
    return jnp.stack(pieces, axis=3)


def block_back(grad_out, inputs, hidden, w_first, w_second):
    act_h = jnp.maximum(hidden, 0)
    act_x = jnp.maximum(inputs, 0)
    grad_z = jnp.einsum(
        "byxkd,kcd->byxc", tap_views(grad_out, -1), w_second, preferred_element_type=jnp.float32
    )
    g_second = jnp.einsum(
        "byxkc,byxd->kcd", tap_views(act_h, 1), grad_out, preferred_element_type=jnp.float32
    )
    grad_h = jnp.where(hidden > 0, grad_z, 0.0).astype(jnp.bfloat16)
    grad_u = jnp.einsum(
        "byxkd,kcd->byxc", tap_views(grad_h, -1), w_first, preferred_element_type=jnp.float32
    )
    g_first = jnp.einsum(
        "byxkc,byxd->kcd", tap_views(act_x, 1), grad_h, preferred_element_type=jnp.float32
    )
    grad_x = (grad_out.astype(jnp.float32) + jnp.where(inputs > 0, grad_u, 0.0)).astype(
        jnp.bfloat16
    )
    return (grad_x, jnp.stack([g_first, g_second]))


def on_device(saved_x, saved_h, kernels, grad_in, loss_grads):
    position = lax.axis_index("section")
    sections_total = lax.axis_size("section")
    bit_count = sections_total.bit_length() - 1
    weights = kernels[0]
    ticks_total = saved_x.shape[1]
    incoming_a = grad_in[0, 0]
    incoming_b = grad_in[1, 0]
    total_a = None
    total_b = None
    for tick_index in range(ticks_total):
        if tick_index > 0:
            from_above = from_behind(out_a, "section", -1)
            from_below = from_behind(out_b, "section", 1)
            incoming_a = jnp.where(
                position == sections_total - 1, loss_grads[0, tick_index - 1], from_above
            )
            incoming_b = jnp.where(position == 0, loss_grads[1, tick_index - 1], from_below)
        out_a, grads_a = block_back(
            incoming_a,
            saved_x[0, tick_index, 0],
            saved_h[0, tick_index, 0],
            weights[0, 0],
            weights[0, 1],
        )
        out_b, grads_b = block_back(
            incoming_b,
            saved_x[1, tick_index, 0],
            saved_h[1, tick_index, 0],
            weights[1, 0],
            weights[1, 1],
        )
        total_a = grads_a if tick_index == 0 else total_a + grads_a
        total_b = grads_b if tick_index == 0 else total_b + grads_b
    channels = total_a.shape[-1]
    grad_a = total_a.reshape(-1, channels)
    grad_b = total_b.reshape(-1, channels)
    extent = saved_x.shape[4]
    factor = 1.0 / float(extent * extent)
    part_a, part_b = (
        lax.psum_scatter(grad_a, "dp", scatter_dimension=0, tiled=True),
        lax.psum_scatter(grad_b, "dp", scatter_dimension=0, tiled=True),
    )
    for bit_number in range(bit_count):
        part_b = from_partner(part_b.astype(jnp.bfloat16), "section", bit_number).astype(
            part_b.dtype
        )
    summed = part_a + part_b
    kernel_grads = (summed * factor)[None]
    edge_grads = jnp.stack([out_a, out_b])[:, None]
    return (kernel_grads, edge_grads)


def solution(mesh):
    return jax.shard_map(
        on_device,
        mesh=mesh,
        in_specs=(
            P(None, None, "section", "dp", None, None, None),
            P(None, None, "section", "dp", None, None, None),
            P("section", None, None, None, None, None),
            P(None, "section", "dp", None, None, None),
            P(None, None, "dp", None, None, None),
        ),
        out_specs=(P("section", "dp", None), P(None, "section", "dp", None, None, None)),
        check_vma=False,
    )
```

profile of v0, /device:TPU:6, one launch (start us, length us, event | category | flops | bytes accessed | tf_op | source)
XLA Modules:
  0.0 275.8 jit_solution(11893479076998873308)
XLA Ops:
  7.2 0.9 slice_bitcast_fusion.24
  8.3 0.9 constant_dynamic-update-slice_fusion.112
  9.3 1.4 fusion.24
  11.3 1.9 collective-permute-start.2
  14.4 3.6 %collective-permute-start = (bf16[1,16,16,128]{3,2,1,0:T(8,128)(2,1)S(1)}, bf16[1,16,16,128]{3,2,1,0:T(8,128)(2,1)S(1)}, u32[]{:S(2)}, u32[]{:S(2)}) collective-permute-start(bf16[1,16,16,128]{3,2,1,0:T(8,128)(2,1)S(1)} %fusion.28), channel_id=1, source_target_pairs={{16,0},{32,16},{48,32},{64,48},{80,64},{96,80},{112,96},{128,112},... | collective-permute-start | bytes 196616 | tf_op jit(solution)/shard_map/ppermute | solution.py:10
  20.3 0.6 constant_dynamic-update-slice_fusion.156
  20.9 0.6 constant_dynamic-update-slice_fusion.155
  22.2 0.6 constant_dynamic-update-slice_fusion.170
  22.8 0.6 constant_dynamic-update-slice_fusion.169
  23.4 0.6 constant_dynamic-update-slice_fusion.168
  24.1 0.7 constant_dynamic-update-slice_fusion.167
  24.7 0.6 constant_dynamic-update-slice_fusion.107
  25.4 0.6 constant_dynamic-update-slice_fusion.106
  26.0 0.6 constant_dynamic-update-slice_fusion.105
  26.6 0.6 constant_dynamic-update-slice_fusion.104
  27.3 0.6 constant_dynamic-update-slice_fusion.71
  27.9 0.6 constant_dynamic-update-slice_fusion.70
  28.6 0.6 constant_dynamic-update-slice_fusion.69
  29.2 0.6 constant_dynamic-update-slice_fusion.68
  29.8 0.6 constant_dynamic-update-slice_fusion.35
  31.1 0.6 constant_dynamic-update-slice_fusion.33
  31.8 0.6 constant_dynamic-update-slice_fusion.32
  32.4 0.6 constant_dynamic-update-slice_fusion.8
  33.0 0.6 constant_dynamic-update-slice_fusion.7
  33.7 0.6 constant_dynamic-update-slice_fusion.6
  34.3 0.6 constant_dynamic-update-slice_fusion.5
  34.9 0.6 constant_dynamic-update-slice_fusion.134
  36.2 0.6 constant_dynamic-update-slice_fusion.132
  36.9 0.7 constant_dynamic-update-slice_fusion.131
  37.5 0.8 constant_dynamic-update-slice_fusion.166
  38.4 0.6 constant_dynamic-update-slice_fusion.3
  39.0 0.7 constant_dynamic-update-slice_fusion.2
  40.3 0.6 constant_dynamic-update-slice_fusion.30
  41.0 0.7 constant_dynamic-update-slice_fusion.29
  41.6 0.7 constant_dynamic-update-slice_fusion.66
  42.3 0.7 constant_dynamic-update-slice_fusion.65
  42.9 0.6 constant_dynamic-update-slice_fusion.64
  43.7 0.7 constant_dynamic-update-slice_fusion.63
  45.6 0.6 constant_dynamic-update-slice_fusion.28
  46.9 0.7 copy-done.17
  48.4 7.4 %collective-permute-start.3 = (bf16[1,16,16,128]{3,2,1,0:T(8,128)(2,1)S(1)}, bf16[1,16,16,128]{3,2,1,0:T(8,128)(2,1)S(1)}, u32[]{:S(2)}, u32[]{:S(2)}) collective-permute-start(bf16[1,16,16,128]{3,2,1,0:T(8,128)(2,1)S(1)} %add_convert_fusion.2), channel_id=1, source_target_pairs={{0,16},{16,32},{32,48},{48,64},{64,80},{80,96},{96,112},{112,128},... | collective-permute-start | bytes 196616 | tf_op jit(solution)/shard_map/ppermute | solution.py:10
  57.0 1.9 collective-permute-start.1
  59.3 8.1 %collective-permute-done.1 = bf16[1,16,16,128]{3,2,1,0:T(8,128)(2,1)S(1)} collective-permute-done((bf16[1,16,16,128]{3,2,1,0:T(8,128)(2,1)S(1)}, bf16[1,16,16,128]{3,2,1,0:T(8,128)(2,1)S(1)}, u32[]{:S(2)}, u32[]{:S(2)}) %collective-permute-start.1) | collective-permute-done | bytes 65568 | tf_op jit(solution)/shard_map/ppermute | solution.py:10
  69.5 1.2 fusion.1
  70.8 0.7 constant_dynamic-update-slice_fusion
  71.9 0.7 copy-done.12
  73.3 0.7 copy-done.11
  74.4 0.7 copy-done.15
  76.3 0.7 copy-done.10
  77.3 1.2 fusion
  79.3 94.9 %reduce-scatter.5.cloned.1.call-done = f32[144,128]{1,0:T(8,128)} async-done(((f32[2304,128]{1,0:T(8,128)}), f32[144,128]{1,0:T(8,128)}) %reduce-scatter.5.cloned.1.call-update) | async-done | bytes 73744 | tf_op jit(solution)/shard_map/reduce_scatter | solution.py:96
  174.2 0.9 convert_element_type.139
  175.1 1.9 collective-permute-start.4
  177.0 1.1 collective-permute-done.4
  178.2 2.8 collective-permute-start.5
  180.9 3.1 %collective-permute-done.5 = bf16[144,128]{1,0:T(8,128)(2,1)S(1)} collective-permute-done((bf16[144,128]{1,0:T(8,128)(2,1)S(1)}, bf16[144,128]{1,0:T(8,128)(2,1)S(1)}, u32[]{:S(2)}, u32[]{:S(2)}) %collective-permute-start.5) | collective-permute-done | bytes 36896 | tf_op jit(solution)/shard_map/ppermute | solution.py:16
  184.0 3.2 %collective-permute-start.6 = (bf16[144,128]{1,0:T(8,128)(2,1)S(1)}, bf16[144,128]{1,0:T(8,128)(2,1)S(1)}, u32[]{:S(2)}, u32[]{:S(2)}) collective-permute-start(bf16[144,128]{1,0:T(8,128)(2,1)S(1)} %collective-permute-done.5), channel_id=1, source_target_pairs={{0,64},{16,80},{32,96},{48,112},{64,0},{80,16},{96,32},{112,48},{1... | collective-permute-start | bytes 110600 | tf_op jit(solution)/shard_map/ppermute | solution.py:16
  187.2 4.1 %collective-permute-done.6 = bf16[144,128]{1,0:T(8,128)(2,1)S(1)} collective-permute-done((bf16[144,128]{1,0:T(8,128)(2,1)S(1)}, bf16[144,128]{1,0:T(8,128)(2,1)S(1)}, u32[]{:S(2)}, u32[]{:S(2)}) %collective-permute-start.6) | collective-permute-done | bytes 36896 | tf_op jit(solution)/shard_map/ppermute | solution.py:16
  191.3 7.5 %collective-permute-start.7 = (bf16[144,128]{1,0:T(8,128)(2,1)S(1)}, bf16[144,128]{1,0:T(8,128)(2,1)S(1)}, u32[]{:S(2)}, u32[]{:S(2)}) collective-permute-start(bf16[144,128]{1,0:T(8,128)(2,1)S(1)} %collective-permute-done.6), channel_id=1, source_target_pairs={{0,128},{16,144},{32,160},{48,176},{64,192},{80,208},{96,224},{112... | collective-permute-start | bytes 110600 | tf_op jit(solution)/shard_map/ppermute | solution.py:16
  199.2 2.0 collective-permute-done.7
  201.2 10.0 %collective-permute-start.8 = (bf16[144,128]{1,0:T(8,128)(2,1)S(1)}, bf16[144,128]{1,0:T(8,128)(2,1)S(1)}, u32[]{:S(2)}, u32[]{:S(2)}) collective-permute-start(bf16[144,128]{1,0:T(8,128)(2,1)S(1)} %collective-permute-done.7), channel_id=1, source_target_pairs={{0,256},{16,272},{32,288},{48,304},{64,320},{80,336},{96,352},{112... | collective-permute-start | bytes 110600 | tf_op jit(solution)/shard_map/ppermute | solution.py:16
  211.2 0.7 maximum_bitcast_fusion
  211.8 55.6 %reduce-scatter.3.cloned.1.call-done = f32[144,128]{1,0:T(8,128)} async-done(((f32[2304,128]{1,0:T(8,128)}), f32[144,128]{1,0:T(8,128)}) %reduce-scatter.3.cloned.1.call-update) | async-done | bytes 73744 | tf_op jit(solution)/shard_map/reduce_scatter | solution.py:95
  267.5 1.5 multiply_bitcast_fusion
  (231 shorter events, 16.8 us)
Async XLA Ops:
  7.2 2.1 copy-start
  7.2 167.0 %reduce-scatter.5.cloned.1.call-start = ((), (), s32[]{:S(2)}) async-start(), calls=%async_computation.3 | async-start | bytes 1253376 | tf_op jit(solution)/shard_map/reduce_scatter | solution.py:96
  9.2 1.7 copy-start.1
  9.2 1.7 copy-start.2
  9.3 1.7 copy-start.16
  11.3 34.9 %collective-permute-start.2 = (bf16[1,16,16,128]{3,2,1,0:T(8,128)(2,1)S(1)}, bf16[1,16,16,128]{3,2,1,0:T(8,128)(2,1)S(1)}, u32[]{:S(2)}, u32[]{:S(2)}) collective-permute-start(bf16[1,16,16,128]{3,2,1,0:T(8,128)(2,1)S(1)} %fusion.29), channel_id=1, source_target_pairs={{0,16},{16,32},{32,48},{48,64},{64,80},{80,96},{96,112},{112,128},... | collective-permute-start | bytes 196616 | tf_op jit(solution)/shard_map/ppermute | solution.py:10
  14.4 31.8 %collective-permute-start = (bf16[1,16,16,128]{3,2,1,0:T(8,128)(2,1)S(1)}, bf16[1,16,16,128]{3,2,1,0:T(8,128)(2,1)S(1)}, u32[]{:S(2)}, u32[]{:S(2)}) collective-permute-start(bf16[1,16,16,128]{3,2,1,0:T(8,128)(2,1)S(1)} %fusion.28), channel_id=1, source_target_pairs={{16,0},{32,16},{48,32},{64,48},{80,64},{96,80},{112,96},{128,112},... | collective-permute-start | bytes 196616 | tf_op jit(solution)/shard_map/ppermute | solution.py:10
  18.9 0.9 copy-start.6
  19.4 0.8 copy-start.4
  26.0 11.5 %copy-start.8 = (bf16[1,16,16,9,128]{4,2,1,3,0:T(8,128)(2,1)S(1)}, bf16[1,16,16,9,128]{4,2,1,3,0:T(8,128)(2,1)}, u32[]{:S(2)}) copy-start(bf16[1,16,16,9,128]{4,2,1,3,0:T(8,128)(2,1)} %constant_dynamic-update-slice_fusion.167) | copy-start | bytes 1769476
  27.3 10.2 %copy-start.9 = (bf16[1,16,16,9,128]{4,2,1,3,0:T(8,128)(2,1)S(1)}, bf16[1,16,16,9,128]{4,2,1,3,0:T(8,128)(2,1)}, u32[]{:S(2)}) copy-start(bf16[1,16,16,9,128]{4,2,1,3,0:T(8,128)(2,1)} %constant_dynamic-update-slice_fusion.104) | copy-start | bytes 1769476
  38.3 5.3 %copy-start.13 = (bf16[1,16,16,9,128]{4,2,1,3,0:T(8,128)(2,1)S(1)}, bf16[1,16,16,9,128]{4,2,1,3,0:T(8,128)(2,1)}, u32[]{:S(2)}) copy-start(bf16[1,16,16,9,128]{4,2,1,3,0:T(8,128)(2,1)} %get-tuple-element.9) | copy-start | bytes 1769476
  44.4 1.1 copy-start.7
  44.4 1.8 copy-start.3
  46.3 1.3 copy-start.17
  48.4 10.9 %collective-permute-start.3 = (bf16[1,16,16,128]{3,2,1,0:T(8,128)(2,1)S(1)}, bf16[1,16,16,128]{3,2,1,0:T(8,128)(2,1)S(1)}, u32[]{:S(2)}, u32[]{:S(2)}) collective-permute-start(bf16[1,16,16,128]{3,2,1,0:T(8,128)(2,1)S(1)} %add_convert_fusion.2), channel_id=1, source_target_pairs={{0,16},{16,32},{32,48},{48,64},{64,80},{80,96},{96,112},{112,128},... | collective-permute-start | bytes 196616 | tf_op jit(solution)/shard_map/ppermute | solution.py:10
  57.0 10.4 %collective-permute-start.1 = (bf16[1,16,16,128]{3,2,1,0:T(8,128)(2,1)S(1)}, bf16[1,16,16,128]{3,2,1,0:T(8,128)(2,1)S(1)}, u32[]{:S(2)}, u32[]{:S(2)}) collective-permute-start(bf16[1,16,16,128]{3,2,1,0:T(8,128)(2,1)S(1)} %add_convert_fusion.3), channel_id=1, source_target_pairs={{16,0},{32,16},{48,32},{64,48},{80,64},{96,80},{112,96},{128,112},... | collective-permute-start | bytes 196616 | tf_op jit(solution)/shard_map/ppermute | solution.py:10
  68.3 0.8 copy-start.14
  70.8 196.7 %reduce-scatter.3.cloned.1.call-start = ((), (), s32[]{:S(2)}) async-start(), calls=%async_computation.2 | async-start | bytes 1253376 | tf_op jit(solution)/shard_map/reduce_scatter | solution.py:95
  71.5 1.1 copy-start.12
  73.0 1.1 copy-start.11
  74.0 1.1 copy-start.15
  74.0 1.5 copy-start.18
  74.4 1.5 copy-start.5
  75.9 1.1 copy-start.10
  175.1 3.1 %collective-permute-start.4 = (bf16[144,128]{1,0:T(8,128)(2,1)S(1)}, bf16[144,128]{1,0:T(8,128)(2,1)S(1)}, u32[]{:S(2)}, u32[]{:S(2)}) collective-permute-start(bf16[144,128]{1,0:T(8,128)(2,1)S(1)} %convert_element_type.139), channel_id=1, source_target_pairs={{0,16},{16,0},{32,48},{48,32},{64,80},{80,64},{96,112},{112,96},{1... | collective-permute-start | bytes 110600 | tf_op jit(solution)/shard_map/ppermute | solution.py:16
  178.2 5.8 %collective-permute-start.5 = (bf16[144,128]{1,0:T(8,128)(2,1)S(1)}, bf16[144,128]{1,0:T(8,128)(2,1)S(1)}, u32[]{:S(2)}, u32[]{:S(2)}) collective-permute-start(bf16[144,128]{1,0:T(8,128)(2,1)S(1)} %collective-permute-done.4), channel_id=1, source_target_pairs={{0,32},{16,48},{32,0},{48,16},{64,96},{80,112},{96,64},{112,80},{1... | collective-permute-start | bytes 110600 | tf_op jit(solution)/shard_map/ppermute | solution.py:16
  184.0 7.3 %collective-permute-start.6 = (bf16[144,128]{1,0:T(8,128)(2,1)S(1)}, bf16[144,128]{1,0:T(8,128)(2,1)S(1)}, u32[]{:S(2)}, u32[]{:S(2)}) collective-permute-start(bf16[144,128]{1,0:T(8,128)(2,1)S(1)} %collective-permute-done.5), channel_id=1, source_target_pairs={{0,64},{16,80},{32,96},{48,112},{64,0},{80,16},{96,32},{112,48},{1... | collective-permute-start | bytes 110600 | tf_op jit(solution)/shard_map/ppermute | solution.py:16
  191.3 9.9 %collective-permute-start.7 = (bf16[144,128]{1,0:T(8,128)(2,1)S(1)}, bf16[144,128]{1,0:T(8,128)(2,1)S(1)}, u32[]{:S(2)}, u32[]{:S(2)}) collective-permute-start(bf16[144,128]{1,0:T(8,128)(2,1)S(1)} %collective-permute-done.6), channel_id=1, source_target_pairs={{0,128},{16,144},{32,160},{48,176},{64,192},{80,208},{96,224},{112... | collective-permute-start | bytes 110600 | tf_op jit(solution)/shard_map/ppermute | solution.py:16
  201.2 66.3 %collective-permute-start.8 = (bf16[144,128]{1,0:T(8,128)(2,1)S(1)}, bf16[144,128]{1,0:T(8,128)(2,1)S(1)}, u32[]{:S(2)}, u32[]{:S(2)}) collective-permute-start(bf16[144,128]{1,0:T(8,128)(2,1)S(1)} %collective-permute-done.7), channel_id=1, source_target_pairs={{0,256},{16,272},{32,288},{48,304},{64,320},{80,336},{96,352},{112... | collective-permute-start | bytes 110600 | tf_op jit(solution)/shard_map/ppermute | solution.py:16
Sparse Core Ops, SparseCore 0:
  70.9 103.2 reduce-scatter.4
  177.0 90.4 reduce-scatter.2
where the time goes:
time: 277 us; the launch traced here: 276 us
  waiting for transfers between devices  169 us (61%)
  starting transfers between devices  40.3 us (15%)
  local copies, waits for them, and re-layouts  35.5 us (13%)
  between operations  15.1 us (5%)
  matrix products  9.37 us (3%)
  other arithmetic  6.57 us (2%)
    reduce_scatter x1, waiting for transfers between devices, on_device(): lax.psum_scatter(grad_b, 'dp', scatter_dimension=0, tiled=True)  94.9 us
    reduce_scatter x1, waiting for transfers between devices, on_device(): lax.psum_scatter(grad_a, 'dp', scatter_dimension=0, tiled=True)  55.6 us
    unnamed x218, local copies, waits for them, and re-layouts  32.7 us
    ppermute x5, starting transfers between devices, from_partner(): return lax.ppermute(value, axis, pairs)  25.3 us
    ppermute x4, starting transfers between devices, from_behind(): return lax.ppermute(value, axis, pairs)  14.9 us
    ppermute x5, waiting for transfers between devices, from_partner(): return lax.ppermute(value, axis, pairs)  10.4 us
    ppermute x4, waiting for transfers between devices, from_behind(): return lax.ppermute(value, axis, pairs)  8.09 us
  transfers between devices with their start and end apart: 11, of which 7 were waited for; matrix products, arithmetic and copies ran while one was open for 13% of the time, Pallas kernels for 0%

commit v1 on v0

v1 whole, which is shorter than its diff:
```python
import functools

import jax
import jax.numpy as jnp
from jax import lax
from jax.experimental import pallas as pl
from jax.experimental.pallas import tpu as pltpu
from jax.sharding import PartitionSpec as P

TAPS = 9
PIECE = 64
VMEM_LIMIT = 16 << 20


def fill_shifts(pad_ref, value, extent):
    cells, channels = value.shape
    wide = value.astype(jnp.float32)
    column = lax.broadcasted_iota(jnp.int32, (cells, channels), 0) & (extent - 1)
    left = jnp.where(column == extent - 1, 0.0, pltpu.roll(wide, cells - 1, 0))
    right = jnp.where(column == 0, 0.0, pltpu.roll(wide, 1, 0))
    edge = jnp.zeros((extent, channels), value.dtype)
    for j, moved in enumerate((left.astype(value.dtype), value, right.astype(value.dtype))):
        pad_ref[j, 0:extent, :] = edge
        pad_ref[j, extent : extent + cells, :] = moved
        pad_ref[j, extent + cells : 2 * extent + cells, :] = edge


def views(pad_ref, extent):
    cells = pad_ref.shape[1] - 2 * extent
    taps = []
    for row in (-1, 0, 1):
        for col in (-1, 0, 1):
            start = (1 - row) * extent
            taps.append(pad_ref[col + 1, start : start + cells, :])
    return jnp.concatenate(taps, axis=1)


def conv_back(pad_ref, w_ref, replica, which, extent):
    weights = jnp.concatenate([w_ref[replica, which, k] for k in range(TAPS)], axis=1)
    return lax.dot_general(
        views(pad_ref, extent),
        weights,
        (((1,), (1,)), ((), ())),
        preferred_element_type=jnp.float32,
    )


def vmem():
    return pl.BlockSpec(memory_space=pltpu.VMEM)


def left_alone():
    return pl.BlockSpec(memory_space=pl.ANY)


def smem():
    return pl.BlockSpec(memory_space=pltpu.SMEM)


def chain_kernel(extent, tick, ticks, slot, packed, info_ref, x_ref, h_ref, w_ref, _, *refs):
    parity = info_ref[0]
    replica = parity if slot == 0 else 1 - parity
    refs = list(refs)
    pad_ref = refs.pop()
    if tick == 0:
        g = refs.pop(0)[replica]
    else:
        g = refs.pop(0)[...]
        if slot == 1:
            loss = refs.pop(0)[replica * (ticks - 1) + tick - 1]
            end = jnp.full(g.shape, info_ref[1], jnp.int32)
            g = jnp.where(end > 0, loss.astype(jnp.float32), g.astype(jnp.float32)).astype(g.dtype)
    first = refs.pop(0)[...] if packed else None
    gh_ref, gx_ref = refs[0], refs[1]
    if tick == 0 or slot == 1:
        refs[2][...] = g
    fill_shifts(pad_ref, g, extent)
    grad_z = conv_back(pad_ref, w_ref, replica, 1, extent)
    h = h_ref[replica * ticks + tick].astype(jnp.float32)
    grad_h = jnp.where(h > 0, grad_z, 0.0).astype(jnp.bfloat16)
    gh_ref[...] = grad_h
    fill_shifts(pad_ref, grad_h, extent)
    grad_u = conv_back(pad_ref, w_ref, replica, 0, extent)
    x = x_ref[replica * ticks + tick].astype(jnp.float32)
    grad_x = (g.astype(jnp.float32) + jnp.where(x > 0, grad_u, 0.0)).astype(jnp.bfloat16)
    if packed:
        gx_ref[replica] = grad_x
        gx_ref[1 - replica] = first
    else:
        gx_ref[...] = grad_x


def chain(info, saved_x, saved_h, weights, after, arrays, slot, tick, ticks, extent, packed):
    cells, channels = saved_x.shape[1:]
    like = jax.ShapeDtypeStruct((cells, channels), jnp.bfloat16)
    out_shape = [like, jax.ShapeDtypeStruct((2, cells, channels), jnp.bfloat16) if packed else like]
    if tick == 0 or slot == 1:
        out_shape.append(like)
    outs = pl.pallas_call(
        functools.partial(chain_kernel, extent, tick, ticks, slot, packed),
        in_specs=[smem()] + [vmem()] * 3 + [left_alone()] + [vmem()] * len(arrays),
        out_specs=[vmem()] * len(out_shape),
        out_shape=out_shape,
        scratch_shapes=[pltpu.VMEM((3, cells + 2 * extent, channels), jnp.bfloat16)],
        compiler_params=pltpu.CompilerParams(vmem_limit_bytes=VMEM_LIMIT),
        cost_estimate=pl.CostEstimate(
            flops=4 * cells * TAPS * channels * channels, bytes_accessed=1000000, transcendentals=0
        ),
        name=f"chain_{slot}_{tick}",
    )(info, saved_x, saved_h, weights, after, *arrays)
    return (outs[2] if len(outs) == 3 else arrays[0]), outs[0], outs[1]


def wgrad_kernel(extent, slot, ticks, at, has_acc, form, info_ref, x_ref, h_ref, *refs):
    parity = info_ref[0]
    replica = parity if slot == 0 else 1 - parity
    count = len(at)
    grads_h, grads = refs[:count], refs[count : 2 * count]
    acc_ref = refs[2 * count] if has_acc else None
    out_ref, pad_ref = refs[-2], refs[-1]
    if form == "both":
        out_ref[:, 0] = refs[2 * count + 1][...]
    for pair, (act_ref, sides) in enumerate(((x_ref, grads_h), (h_ref, grads))):
        rows, columns = [], []
        for n, tick in enumerate(at):
            fill_shifts(pad_ref.at[pair, n], sides[n][...], extent)
            columns.append(views(pad_ref.at[pair, n], extent))
            act = act_ref[replica * ticks + tick].astype(jnp.float32)
            rows.append(jnp.maximum(act, 0.0).astype(jnp.bfloat16))
        left = rows[0] if count == 1 else jnp.concatenate(rows, axis=0)
        right = columns[0] if count == 1 else jnp.concatenate(columns, axis=0)
        total = lax.dot_general(
            left, right, (((0,), (0,)), ((), ())), preferred_element_type=jnp.float32
        )
        channels = left.shape[1]
        for k in range(TAPS):
            for start in range(0, channels, PIECE):
                piece = total[start : start + PIECE, k * channels : (k + 1) * channels]
                row = (pair * TAPS + k) * channels + start
                if has_acc:
                    piece = piece + acc_ref[row : row + PIECE, :]
                if form == "flat":
                    out_ref[row : row + PIECE, :] = piece
                    continue
                rows_each = out_ref.shape[-2]
                part, inner = row // rows_each, row % rows_each
                at_part = (part, slot) if form == "both" else (part,)
                out_ref[*at_part, inner : inner + PIECE, :] = piece.astype(out_ref.dtype)


def wgrad(info, saved_x, saved_h, grads_h, grads, at, more, slot, ticks, extent, parts, form):
    cells, channels = saved_x.shape[1:]
    rows = 2 * TAPS * channels
    shape = {
        "flat": (rows, channels),
        "parts": (parts, rows // parts, channels),
        "both": (parts, 2, rows // parts, channels),
    }[form]
    out_shape = jax.ShapeDtypeStruct(shape, jnp.float32 if form == "flat" else jnp.bfloat16)
    args = [*grads_h, *grads, *more]
    return pl.pallas_call(
        functools.partial(wgrad_kernel, extent, slot, ticks, at, len(more) > 0, form),
        in_specs=[smem()] + [vmem()] * (2 + len(args)),
        out_specs=vmem(),
        out_shape=out_shape,
        scratch_shapes=[pltpu.VMEM((2, len(at), 3, cells + 2 * extent, channels), jnp.bfloat16)],
        compiler_params=pltpu.CompilerParams(vmem_limit_bytes=VMEM_LIMIT),
        cost_estimate=pl.CostEstimate(
            flops=4 * len(at) * cells * TAPS * channels * channels,
            bytes_accessed=2000000,
            transcendentals=0,
        ),
        name=f"wgrad_{slot}_" + "".join(str(t) for t in at),
    )(info, saved_x, saved_h, *args)


def exchange(value, offset):
    total = lax.axis_size("section")
    pairs = []
    for low in range(offset, total - 1, 2):
        pairs += [(low, low + 1), (low + 1, low)]
    return lax.ppermute(value, "section", pairs)


def on_device(factors, saved_x, saved_h, kernels, grad_in, loss_grads):
    ticks = saved_x.shape[1]
    extent, channels = saved_x.shape[4], saved_x.shape[6]
    cells = extent * extent
    sections = lax.axis_size("section")
    outer, inner = factors
    position = lax.axis_index("section")
    parity = position % 2
    at_end = (position == 0) | (position == sections - 1)
    info = jnp.stack([parity, at_end.astype(jnp.int32)]).astype(jnp.int32)
    weights = kernels[0]
    xs = saved_x.reshape(-1, cells, channels)
    hs = saved_h.reshape(-1, cells, channels)
    start = grad_in.reshape(-1, cells, channels)
    loss = loss_grads.reshape(-1, cells, channels)

    run = functools.partial(chain, info, xs, hs, weights, ticks=ticks, extent=extent)
    sums = functools.partial(wgrad, info, xs, hs, ticks=ticks, extent=extent, parts=outer)
    g, gh = [[], []], [[], []]
    arrivals = [None, None]
    out = [None, None]
    after = start
    for tick in range(ticks):
        last = tick == ticks - 1
        for slot in (0, 1):
            if tick == 0:
                arrays = [start]
            elif slot == 0:
                arrays = [arrivals[0]]
            else:
                arrays = [arrivals[1], loss]
            packed = last and slot == 1
            if packed:
                slot0 = sums(gh[0], g[0], tuple(range(ticks)), [], slot=0, form="parts")
                after = slot0
                arrays.append(out[0])
            g_now, gh_now, out[slot] = run(after, arrays, slot=slot, tick=tick, packed=packed)
            after = gh_now
            g[slot].append(g_now)
            gh[slot].append(gh_now)
            if not last:
                if slot == 0:
                    next_one = exchange(out[0], 1)
                else:
                    arrivals = [exchange(out[1], 0), next_one]
    edge_grads = out[1].reshape(2, 1, 1, extent, extent, channels)

    early = tuple(range(ticks - 1))
    part1 = sums(gh[1][:-1], g[1][:-1], early, [], slot=1, form="flat")
    both = sums(gh[1][-1:], g[1][-1:], (ticks - 1,), [part1, slot0], slot=1, form="both")

    rows = both.shape[2]
    across = [[i * inner + j for i in range(outer)] for j in range(inner)]
    along = [[i * inner + j for j in range(inner)] for i in range(outer)]

    def total(value):
        parts = [value[n].astype(jnp.float32) for n in range(value.shape[0])]
        return functools.reduce(lambda a, b: a + b, parts)

    both = lax.all_to_all(both, "dp", 0, 0, axis_index_groups=across, tiled=True)
    summed = total(both)
    mine = jnp.where(parity == 0, summed[0], summed[1]).astype(jnp.bfloat16)
    other = jnp.where(parity == 0, summed[1], summed[0]).astype(jnp.bfloat16)

    def finish(value):
        value = value.reshape(inner, rows // inner, channels)
        return total(lax.all_to_all(value, "dp", 0, 0, axis_index_groups=along, tiled=True))

    other = finish(other).astype(jnp.bfloat16)
    mirror = [(i, sections - 1 - i) for i in range(sections)]
    other = lax.ppermute(other, "section", mirror)
    mine = finish(mine)
    factor = 1.0 / float(cells)
    kernel_grads = ((mine + other.astype(jnp.float32)) * factor)[None]
    return (kernel_grads, edge_grads)


def solution(mesh):
    shards = mesh.shape["dp"]
    outer = next(f for f in (4, 2, 1) if shards % f == 0)
    return jax.shard_map(
        functools.partial(on_device, (outer, shards // outer)),
        mesh=mesh,
        in_specs=(
            P(None, None, "section", "dp", None, None, None),
            P(None, None, "section", "dp", None, None, None),
            P("section", None, None, None, None, None),
            P(None, "section", "dp", None, None, None),
            P(None, None, "dp", None, None, None),
        ),
        out_specs=(P("section", "dp", None), P(None, "section", "dp", None, None, None)),
        check_vma=False,
    )
```

time: 277 us -> 91.6 us (0.33)
  the two profiles are of different devices: /device:TPU:6 before, /device:TPU:39 now
where the time goes in v1:
time: 91.6 us; the launch traced here: 91 us
  starting transfers between devices  47.1 us (51%)
  waiting for transfers between devices  14.5 us (16%)
  Pallas kernels  13.2 us (14%)
  blocking collectives  9.75 us (11%)
  local copies, waits for them, and re-layouts  4.18 us (5%)
  other arithmetic  1.6 us (2%)
    ppermute x4, starting transfers between devices, exchange(): return lax.ppermute(value, 'section', pairs)  22.3 us
    ppermute x1, starting transfers between devices, on_device(): other = lax.ppermute(other, 'section', mirror)  16.2 us
    all_to_all x1, waiting for transfers between devices, on_device(): lax.all_to_all(both, 'dp', 0, 0, axis_index_groups=across, tiled=True)  11 us
    all_to_all x1, blocking collectives, finish(): lax.all_to_all(value, 'dp', 0, 0, axis_index_groups=along, tiled=True)  9.75 us
    pallas_call x6, Pallas kernels, chain(): pl.pallas_call(functools.partial(chain_kernel, extent, tick, ticks, slot,...  8.68 us
    pallas_call x3, Pallas kernels, wgrad(): pl.pallas_call(functools.partial(wgrad_kernel, extent, slot, ticks, at, l...  4.48 us
    all_to_all x1, starting transfers between devices, finish(): lax.all_to_all(value, 'dp', 0, 0, axis_index_groups=along, tiled=True)  4.4 us
    all_to_all x1, starting transfers between devices, on_device(): lax.all_to_all(both, 'dp', 0, 0, axis_index_groups=across, tiled=True)  4.18 us
  transfers between devices with their start and end apart: 7, of which 3 were waited for; matrix products, arithmetic and copies ran while one was open for 0% of the time, Pallas kernels for 6%

profile of v1, /device:TPU:39, one launch (start us, length us, event | category | flops | bytes accessed | tf_op | source)
XLA Modules:
  0.0 91.0 jit_solution(6307720255993264858)
XLA Ops:
  0.6 0.1 pad_add_fusion.info_ref
  0.7 0.0 copy-start
  0.7 1.3 %copy-done = bf16[1,2,2,9,128,128]{5,4,3,2,1,0:T(8,128)(2,1)S(1)} copy-done((bf16[1,2,2,9,128,128]{5,4,3,2,1,0:T(8,128)(2,1)S(1)}, bf16[1,2,2,9,128,128]{5,4,3,2,1,0:T(8,128)(2,1)}, u32[]{:S(2)}) %copy-start) | copy-done | bytes 1179672
  2.0 0.0 copy-start.2
  2.0 1.0 %copy-done.2 = bf16[2,3,1,1,16,16,128]{6,5,4,3,2,1,0:T(8,128)(2,1)S(1)} copy-done((bf16[2,3,1,1,16,16,128]{6,5,4,3,2,1,0:T(8,128)(2,1)S(1)}, bf16[2,3,1,1,16,16,128]{6,5,4,3,2,1,0:T(8,128)(2,1)}, u32[]{:S(2)}) %copy-start.2) | copy-done | bytes 393240
  3.0 0.0 copy-start.3
  3.0 1.0 %copy-done.3 = bf16[2,3,1,1,16,16,128]{6,5,4,3,2,1,0:T(8,128)(2,1)S(1)} copy-done((bf16[2,3,1,1,16,16,128]{6,5,4,3,2,1,0:T(8,128)(2,1)S(1)}, bf16[2,3,1,1,16,16,128]{6,5,4,3,2,1,0:T(8,128)(2,1)}, u32[]{:S(2)}) %copy-start.3) | copy-done | bytes 393240
  4.0 0.0 copy-start.4
  4.0 0.9 copy-done.4
  4.9 1.3 %chain_0_0.1 = (bf16[256,128]{1,0:T(8,128)(2,1)S(1)}, bf16[256,128]{1,0:T(8,128)(2,1)S(1)}, bf16[256,128]{1,0:T(8,128)(2,1)S(1)}) custom-call(s32[2]{0:T(128)S(1)} %pad_add_fusion.info_ref, bf16[6,256,128]{2,1,0:T(8,128)(2,1)S(1)} %bitcast.28, bf16[6,256,128]{2,1,0:T(8,128)(2,1)S(1)} %bitcast.37, bf16[2,2,9,128,128]{4,3,2,1,0:T(8,128)(2,1)S(1)} %bitcast.22, ...), custom_call_target="tpu_custom_call" | custom-call | flops 150994944 | bytes 1000000 | tf_op jit(solution)/shard_map/chain_0_0/pallas_call | solution.py:99
  6.2 1.3 %chain_1_0.1 = (bf16[256,128]{1,0:T(8,128)(2,1)S(1)}, bf16[256,128]{1,0:T(8,128)(2,1)S(1)}, bf16[256,128]{1,0:T(8,128)(2,1)S(1)}) custom-call(s32[2]{0:T(128)S(1)} %pad_add_fusion.info_ref, bf16[6,256,128]{2,1,0:T(8,128)(2,1)S(1)} %bitcast.29, bf16[6,256,128]{2,1,0:T(8,128)(2,1)S(1)} %bitcast.38, bf16[2,2,9,128,128]{4,3,2,1,0:T(8,128)(2,1)S(1)} %bitcast.23, ...), custom_call_target="tpu_custom_call" | custom-call | flops 150994944 | bytes 1000000 | tf_op jit(solution)/shard_map/chain_1_0/pallas_call | solution.py:99
  7.6 0.0 copy-start.5
  7.6 2.7 %collective-permute-start = (bf16[256,128]{1,0:T(8,128)(2,1)S(1)}, bf16[256,128]{1,0:T(8,128)(2,1)S(1)}, u32[]{:S(2)}, u32[]{:S(2)}) collective-permute-start(bf16[256,128]{1,0:T(8,128)(2,1)S(1)} %get-tuple-element.20), channel_id=1, source_target_pairs={{0,16},{16,0},{32,48},{48,32},{64,80},{80,64},{96,112},{112,96},{1... | collective-permute-start | bytes 196616 | tf_op jit(solution)/shard_map/ppermute | solution.py:182
  10.3 8.6 %collective-permute-start.1 = (bf16[256,128]{1,0:T(8,128)(2,1)S(1)}, bf16[256,128]{1,0:T(8,128)(2,1)S(1)}, u32[]{:S(2)}, u32[]{:S(2)}) collective-permute-start(bf16[256,128]{1,0:T(8,128)(2,1)S(1)} %get-tuple-element.22), channel_id=1, source_target_pairs={{16,32},{32,16},{48,64},{64,48},{80,96},{96,80},{112,128},{128,112... | collective-permute-start | bytes 196616 | tf_op jit(solution)/shard_map/ppermute | solution.py:182
  18.9 0.0 collective-permute-done.refs_0_.refs_4_
  19.0 1.3 %chain_0_1.1 = (bf16[256,128]{1,0:T(8,128)(2,1)S(1)}, bf16[256,128]{1,0:T(8,128)(2,1)S(1)}) custom-call(s32[2]{0:T(128)S(1)} %pad_add_fusion.info_ref, bf16[6,256,128]{2,1,0:T(8,128)(2,1)S(1)} %bitcast.30, bf16[6,256,128]{2,1,0:T(8,128)(2,1)S(1)} %bitcast.39, bf16[2,2,9,128,128]{4,3,2,1,0:T(8,128)(2,1)S(1)} %bitcast.24, ...), custom_call_target="tpu_custom_call" | custom-call | flops 150994944 | bytes 1000000 | tf_op jit(solution)/shard_map/chain_0_1/pallas_call | solution.py:99
  20.3 1.6 %collective-permute-done.1.refs_0_ = bf16[256,128]{1,0:T(8,128)(2,1)S(1)} collective-permute-done((bf16[256,128]{1,0:T(8,128)(2,1)S(1)}, bf16[256,128]{1,0:T(8,128)(2,1)S(1)}, u32[]{:S(2)}, u32[]{:S(2)}) %collective-permute-start.1) | collective-permute-done | bytes 65568 | tf_op jit(solution)/shard_map/ppermute | solution.py:182
  21.9 0.0 copy-done.5
  21.9 1.3 %chain_1_1.1 = (bf16[256,128]{1,0:T(8,128)(2,1)S(1)}, bf16[256,128]{1,0:T(8,128)(2,1)S(1)}, bf16[256,128]{1,0:T(8,128)(2,1)S(1)}) custom-call(s32[2]{0:T(128)S(1)} %pad_add_fusion.info_ref, bf16[6,256,128]{2,1,0:T(8,128)(2,1)S(1)} %bitcast.31, bf16[6,256,128]{2,1,0:T(8,128)(2,1)S(1)} %bitcast.40, bf16[2,2,9,128,128]{4,3,2,1,0:T(8,128)(2,1)S(1)} %bitcast.25, ...), custom_call_target="tpu_custom_call" | custom-call | flops 150994944 | bytes 1000000 | tf_op jit(solution)/shard_map/chain_1_1/pallas_call | solution.py:99
  23.3 0.0 copy-start.1
  23.3 2.1 %collective-permute-start.2 = (bf16[256,128]{1,0:T(8,128)(2,1)S(1)}, bf16[256,128]{1,0:T(8,128)(2,1)S(1)}, u32[]{:S(2)}, u32[]{:S(2)}) collective-permute-start(bf16[256,128]{1,0:T(8,128)(2,1)S(1)} %get-tuple-element.24), channel_id=1, source_target_pairs={{0,16},{16,0},{32,48},{48,32},{64,80},{80,64},{96,112},{112,96},{1... | collective-permute-start | bytes 196616 | tf_op jit(solution)/shard_map/ppermute | solution.py:182
  25.3 8.9 %collective-permute-start.3 = (bf16[256,128]{1,0:T(8,128)(2,1)S(1)}, bf16[256,128]{1,0:T(8,128)(2,1)S(1)}, u32[]{:S(2)}, u32[]{:S(2)}) collective-permute-start(bf16[256,128]{1,0:T(8,128)(2,1)S(1)} %get-tuple-element.27), channel_id=1, source_target_pairs={{16,32},{32,16},{48,64},{64,48},{80,96},{96,80},{112,128},{128,112... | collective-permute-start | bytes 196616 | tf_op jit(solution)/shard_map/ppermute | solution.py:182
  34.3 1.1 %wgrad_1_01.1.refs_2_ = f32[2304,128]{1,0:T(8,128)S(1)} custom-call(s32[2]{0:T(128)S(1)} %pad_add_fusion.info_ref, bf16[6,256,128]{2,1,0:T(8,128)(2,1)S(1)} %bitcast.32, bf16[6,256,128]{2,1,0:T(8,128)(2,1)S(1)} %bitcast.41, bf16[256,128]{1,0:T(8,128)(2,1)S(1)} %get-tuple-element.19._.refs_0_, bf16[256,128]{1,0:T(8,128)(2,1)S(1)} %get-tuple-element.23._.refs_1_, ...), custom_call_target="tpu_custom_call" | custom-call | flops 301989888 | bytes 2000000 | tf_op jit(solution)/shard_map/wgrad_1_01/pallas_call | solution.py:161
  35.4 0.0 collective-permute-done.2.refs_0_.refs_5_
  35.4 0.0 copy-done.1
  35.4 1.3 %chain_0_2.1 = (bf16[256,128]{1,0:T(8,128)(2,1)S(1)}, bf16[256,128]{1,0:T(8,128)(2,1)S(1)}) custom-call(s32[2]{0:T(128)S(1)} %pad_add_fusion.info_ref, bf16[6,256,128]{2,1,0:T(8,128)(2,1)S(1)} %bitcast.33, bf16[6,256,128]{2,1,0:T(8,128)(2,1)S(1)} %bitcast.42, bf16[2,2,9,128,128]{4,3,2,1,0:T(8,128)(2,1)S(1)} %bitcast.26, ...), custom_call_target="tpu_custom_call" | custom-call | flops 150994944 | bytes 1000000 | tf_op jit(solution)/shard_map/chain_0_2/pallas_call | solution.py:99
  36.8 1.4 %wgrad_0_012.1._.refs_3_ = bf16[4,576,128]{2,1,0:T(8,128)(2,1)S(1)} custom-call(s32[2]{0:T(128)S(1)} %pad_add_fusion.info_ref, bf16[6,256,128]{2,1,0:T(8,128)(2,1)S(1)} %bitcast.34, bf16[6,256,128]{2,1,0:T(8,128)(2,1)S(1)} %bitcast.43, bf16[256,128]{1,0:T(8,128)(2,1)S(1)} %get-tuple-element.18._.refs_0_, bf16[256,128]{1,0:T(8,128)(2,1)S(1)} %get-tuple-element.21._.refs_1_, ...), custom_call_target="tpu_custom_call" | custom-call | flops 452984832 | bytes 2000000 | tf_op jit(solution)/shard_map/wgrad_0_012/pallas_call | solution.py:161
  38.1 0.0 collective-permute-done.3.refs_0_
  38.1 2.0 %chain_1_2.1 = (bf16[256,128]{1,0:T(8,128)(2,1)S(1)}, bf16[2,256,128]{2,1,0:T(8,128)(2,1)}, bf16[256,128]{1,0:T(8,128)(2,1)S(1)}) custom-call(s32[2]{0:T(128)S(1)} %pad_add_fusion.info_ref, bf16[6,256,128]{2,1,0:T(8,128)(2,1)S(1)} %bitcast.35, bf16[6,256,128]{2,1,0:T(8,128)(2,1)S(1)} %bitcast.44, bf16[2,2,9,128,128]{4,3,2,1,0:T(8,128)(2,1)S(1)} %bitcast.27, ...), custom_call_target="tpu_custom_call" | custom-call | flops 150994944 | bytes 1000000 | tf_op jit(solution)/shard_map/chain_1_2/pallas_call | solution.py:99
  40.1 2.0 %wgrad_1_2.1 = bf16[4,2,576,128]{3,2,1,0:T(8,128)(2,1)} custom-call(s32[2]{0:T(128)S(1)} %pad_add_fusion.info_ref, bf16[6,256,128]{2,1,0:T(8,128)(2,1)S(1)} %bitcast.36, bf16[6,256,128]{2,1,0:T(8,128)(2,1)S(1)} %bitcast.45, bf16[256,128]{1,0:T(8,128)(2,1)S(1)} %get-tuple-element.29.refs_0_, bf16[256,128]{1,0:T(8,128)(2,1)S(1)} %get-tuple-element.30.refs_1_, ...), custom_call_target="tpu_custom_call" | custom-call | flops 150994944 | bytes 2000000 | tf_op jit(solution)/shard_map/wgrad_1_2/pallas_call | solution.py:161
  42.1 4.2 %all-to-all-start = ((bf16[4,2,576,128]{3,2,1,0:T(8,128)(2,1)}), bf16[4,2,576,128]{3,2,1,0:T(8,128)(2,1)S(1)}, u32[]{:S(2)}, u32[]{:S(2)}) async-start(bf16[4,2,576,128]{3,2,1,0:T(8,128)(2,1)} %wgrad_1_2.1), calls=%async_computation | async-start | bytes 2359296 | tf_op jit(solution)/shard_map/all_to_all | solution.py:244
  46.3 11.0 %all-to-all-done = bf16[4,2,576,128]{3,2,1,0:T(8,128)(2,1)S(1)} async-done(((bf16[4,2,576,128]{3,2,1,0:T(8,128)(2,1)}), bf16[4,2,576,128]{3,2,1,0:T(8,128)(2,1)S(1)}, u32[]{:S(2)}, u32[]{:S(2)}) %all-to-all-start) | async-done | bytes 1179680 | tf_op jit(solution)/shard_map/all_to_all | solution.py:244
  57.3 0.2 convert_add_fusion
  57.5 0.7 select_convert_fusion.1
  58.2 9.8 %all_to_all.15 = bf16[4,144,128]{2,1,0:T(8,128)(2,1)S(1)} all-to-all(bf16[4,144,128]{2,1,0:T(8,128)(2,1)S(1)} %bitcast.51), channel_id=1, replica_groups={{0,1,2,3},{4,5,6,7},{8,9,10,11},{12,13,14,15},{16,17,18,19},{20,21,22,2..., dimensions={0} | all-to-all | bytes 294912 | tf_op jit(solution)/shard_map/all_to_all | solution.py:251
  67.9 4.4 %all-to-all-start.1 = ((bf16[4,144,128]{2,1,0:T(8,128)(2,1)}), bf16[4,144,128]{2,1,0:T(8,128)(2,1)S(1)}, u32[]{:S(2)}, u32[]{:S(2)}) async-start(bf16[4,144,128]{2,1,0:T(8,128)(2,1)} %bitcast.7), calls=%async_computation.1 | async-start | bytes 294912 | tf_op jit(solution)/shard_map/all_to_all | solution.py:251
  72.3 16.2 %collective-permute-start.4 = (bf16[144,128]{1,0:T(8,128)(2,1)S(1)}, bf16[144,128]{1,0:T(8,128)(2,1)S(1)}, u32[]{:S(2)}, u32[]{:S(2)}) collective-permute-start(bf16[144,128]{1,0:T(8,128)(2,1)S(1)} %fusion.2), channel_id=1, source_target_pairs={{0,496},{16,480},{32,464},{48,448},{64,432},{80,416},{96,400},{112... | collective-permute-start | bytes 110600 | tf_op jit(solution)/shard_map/ppermute | solution.py:255
  88.5 0.0 all-to-all-done.1
  88.5 1.9 %collective-permute-done.4 = bf16[144,128]{1,0:T(8,128)(2,1)S(1)} collective-permute-done((bf16[144,128]{1,0:T(8,128)(2,1)S(1)}, bf16[144,128]{1,0:T(8,128)(2,1)S(1)}, u32[]{:S(2)}, u32[]{:S(2)}) %collective-permute-start.4) | collective-permute-done | bytes 36896 | tf_op jit(solution)/shard_map/ppermute | solution.py:255
  90.4 0.7 fusion.1
  (1 shorter events, 0.0 us)
Async XLA Ops:
  0.7 1.3 %copy-start = (bf16[1,2,2,9,128,128]{5,4,3,2,1,0:T(8,128)(2,1)S(1)}, bf16[1,2,2,9,128,128]{5,4,3,2,1,0:T(8,128)(2,1)}, u32[]{:S(2)}) copy-start(bf16[1,2,2,9,128,128]{5,4,3,2,1,0:T(8,128)(2,1)} %param.7) | copy-start | bytes 3538948
  2.0 1.0 %copy-start.2 = (bf16[2,3,1,1,16,16,128]{6,5,4,3,2,1,0:T(8,128)(2,1)S(1)}, bf16[2,3,1,1,16,16,128]{6,5,4,3,2,1,0:T(8,128)(2,1)}, u32[]{:S(2)}) copy-start(bf16[2,3,1,1,16,16,128]{6,5,4,3,2,1,0:T(8,128)(2,1)} %param.5) | copy-start | bytes 1179652
  3.0 1.0 %copy-start.3 = (bf16[2,3,1,1,16,16,128]{6,5,4,3,2,1,0:T(8,128)(2,1)S(1)}, bf16[2,3,1,1,16,16,128]{6,5,4,3,2,1,0:T(8,128)(2,1)}, u32[]{:S(2)}) copy-start(bf16[2,3,1,1,16,16,128]{6,5,4,3,2,1,0:T(8,128)(2,1)} %param.6) | copy-start | bytes 1179652
  4.0 0.9 copy-start.4
  7.6 14.3 %copy-start.5 = (bf16[2,2,1,16,16,128]{5,4,3,2,1,0:T(8,128)(2,1)S(1)}, bf16[2,2,1,16,16,128]{5,4,3,2,1,0:T(8,128)(2,1)}, u32[]{:S(2)}) copy-start(bf16[2,2,1,16,16,128]{5,4,3,2,1,0:T(8,128)(2,1)} %param.9) | copy-start | bytes 786436
  7.6 11.4 %collective-permute-start = (bf16[256,128]{1,0:T(8,128)(2,1)S(1)}, bf16[256,128]{1,0:T(8,128)(2,1)S(1)}, u32[]{:S(2)}, u32[]{:S(2)}) collective-permute-start(bf16[256,128]{1,0:T(8,128)(2,1)S(1)} %get-tuple-element.20), channel_id=1, source_target_pairs={{0,16},{16,0},{32,48},{48,32},{64,80},{80,64},{96,112},{112,96},{1... | collective-permute-start | bytes 196616 | tf_op jit(solution)/shard_map/ppermute | solution.py:182
  10.3 11.6 %collective-permute-start.1 = (bf16[256,128]{1,0:T(8,128)(2,1)S(1)}, bf16[256,128]{1,0:T(8,128)(2,1)S(1)}, u32[]{:S(2)}, u32[]{:S(2)}) collective-permute-start(bf16[256,128]{1,0:T(8,128)(2,1)S(1)} %get-tuple-element.22), channel_id=1, source_target_pairs={{16,32},{32,16},{48,64},{64,48},{80,96},{96,80},{112,128},{128,112... | collective-permute-start | bytes 196616 | tf_op jit(solution)/shard_map/ppermute | solution.py:182
  23.3 12.2 %copy-start.1 = (bf16[1,2,2,9,128,128]{5,4,3,2,1,0:T(8,128)(2,1)S(1)}, bf16[1,2,2,9,128,128]{5,4,3,2,1,0:T(8,128)(2,1)}, u32[]{:S(2)}) copy-start(bf16[1,2,2,9,128,128]{5,4,3,2,1,0:T(8,128)(2,1)} %param.7) | copy-start | bytes 3538948
  23.3 12.1 %collective-permute-start.2 = (bf16[256,128]{1,0:T(8,128)(2,1)S(1)}, bf16[256,128]{1,0:T(8,128)(2,1)S(1)}, u32[]{:S(2)}, u32[]{:S(2)}) collective-permute-start(bf16[256,128]{1,0:T(8,128)(2,1)S(1)} %get-tuple-element.24), channel_id=1, source_target_pairs={{0,16},{16,0},{32,48},{48,32},{64,80},{80,64},{96,112},{112,96},{1... | collective-permute-start | bytes 196616 | tf_op jit(solution)/shard_map/ppermute | solution.py:182
  25.3 12.8 %collective-permute-start.3 = (bf16[256,128]{1,0:T(8,128)(2,1)S(1)}, bf16[256,128]{1,0:T(8,128)(2,1)S(1)}, u32[]{:S(2)}, u32[]{:S(2)}) collective-permute-start(bf16[256,128]{1,0:T(8,128)(2,1)S(1)} %get-tuple-element.27), channel_id=1, source_target_pairs={{16,32},{32,16},{48,64},{64,48},{80,96},{96,80},{112,128},{128,112... | collective-permute-start | bytes 196616 | tf_op jit(solution)/shard_map/ppermute | solution.py:182
  42.1 15.2 %all-to-all-start = ((bf16[4,2,576,128]{3,2,1,0:T(8,128)(2,1)}), bf16[4,2,576,128]{3,2,1,0:T(8,128)(2,1)S(1)}, u32[]{:S(2)}, u32[]{:S(2)}) async-start(bf16[4,2,576,128]{3,2,1,0:T(8,128)(2,1)} %wgrad_1_2.1), calls=%async_computation | async-start | bytes 2359296 | tf_op jit(solution)/shard_map/all_to_all | solution.py:244
  67.9 20.6 %all-to-all-start.1 = ((bf16[4,144,128]{2,1,0:T(8,128)(2,1)}), bf16[4,144,128]{2,1,0:T(8,128)(2,1)S(1)}, u32[]{:S(2)}, u32[]{:S(2)}) async-start(bf16[4,144,128]{2,1,0:T(8,128)(2,1)} %bitcast.7), calls=%async_computation.1 | async-start | bytes 294912 | tf_op jit(solution)/shard_map/all_to_all | solution.py:251
  72.3 18.1 %collective-permute-start.4 = (bf16[144,128]{1,0:T(8,128)(2,1)S(1)}, bf16[144,128]{1,0:T(8,128)(2,1)S(1)}, u32[]{:S(2)}, u32[]{:S(2)}) collective-permute-start(bf16[144,128]{1,0:T(8,128)(2,1)S(1)} %fusion.2), channel_id=1, source_target_pairs={{0,496},{16,480},{32,464},{48,448},{64,432},{80,416},{96,400},{112... | collective-permute-start | bytes 110600 | tf_op jit(solution)/shard_map/ppermute | solution.py:255

commit v2 on v0

v2 whole, which is shorter than its diff:
```python
import functools

import jax
import jax.numpy as jnp
from jax import lax
from jax.experimental import pallas as pl
from jax.experimental.pallas import tpu as pltpu
from jax.sharding import PartitionSpec as P


TAPS = 9
PIECE = 64
PARAMS = pltpu.CompilerParams(vmem_limit_bytes=16 << 20)
BF16, F32 = jnp.bfloat16, jnp.float32


def fill_shifts(pad_ref, value, extent):
    cells, channels = value.shape
    wide = value.astype(F32)
    column = lax.broadcasted_iota(jnp.int32, (cells, channels), 0) & (extent - 1)
    left = jnp.where(column == extent - 1, 0.0, pltpu.roll(wide, cells - 1, 0))
    right = jnp.where(column == 0, 0.0, pltpu.roll(wide, 1, 0))
    edge = jnp.zeros((extent, channels), value.dtype)
    for j, moved in enumerate((left.astype(value.dtype), value, right.astype(value.dtype))):
        pad_ref[j, 0:extent, :] = edge
        pad_ref[j, extent : extent + cells, :] = moved
        pad_ref[j, extent + cells : 2 * extent + cells, :] = edge


def views(pad_ref, extent):
    cells = pad_ref.shape[1] - 2 * extent
    taps = []
    for row in (-1, 0, 1):
        for col in (-1, 0, 1):
            start = (1 - row) * extent
            taps.append(pad_ref[col + 1, start : start + cells, :])
    return jnp.concatenate(taps, axis=1)


def conv_back(pad_ref, w_ref, extent):
    weights = jnp.concatenate([w_ref[k] for k in range(TAPS)], axis=1)
    return lax.dot_general(
        views(pad_ref, extent), weights, (((1,), (1,)), ((), ())), preferred_element_type=F32
    )


def step(g, x_ref, h_ref, w_ref, pad_g, pad_gh, extent):
    fill_shifts(pad_g, g, extent)
    grad_z = conv_back(pad_g, w_ref.at[1], extent)
    grad_h = jnp.where(h_ref[...].astype(F32) > 0, grad_z, 0.0).astype(BF16)
    fill_shifts(pad_gh, grad_h, extent)
    grad_u = conv_back(pad_gh, w_ref.at[0], extent)
    moved = jnp.where(x_ref[...].astype(F32) > 0, grad_u, 0.0)
    return grad_h, (g.astype(F32) + moved).astype(BF16)


def kernel_sums(act_refs, pads, extent):
    rows = [jnp.maximum(a[...].astype(F32), 0.0).astype(BF16) for a in act_refs]
    columns = [views(pad, extent) for pad in pads]
    return lax.dot_general(
        jnp.concatenate(rows, axis=0),
        jnp.concatenate(columns, axis=0),
        (((0,), (0,)), ((), ())),
        preferred_element_type=F32,
    )


def pieces(total, pair):
    channels = total.shape[0]
    for k in range(TAPS):
        for start in range(0, channels, PIECE):
            row = (pair * TAPS + k) * channels + start
            yield row, total[start : start + PIECE, k * channels : (k + 1) * channels]


def first_kernel(extent, ticks, x_hbm, h_hbm, w_hbm, g_hbm, l_hbm, *refs):
    xs, hs, ws, loss, g0, g1, gh0, gh1, gx0, gx1, pads, sems = refs
    gs = (g0, g1)
    position = lax.axis_index("section")
    parity = position & 1
    at_end = (position == 0) | (position == lax.axis_size("section") - 1)
    copies = []

    def fetch(source, target):
        copy = pltpu.make_async_copy(source, target, sems.at[len(copies)])
        copy.start()
        copies.append(copy)

    for slot in (0, 1):
        replica = parity if slot == 0 else 1 - parity
        fetch(g_hbm.at[replica], gs[slot])
        fetch(w_hbm.at[replica, 1], ws.at[slot, 1])
        fetch(h_hbm.at[pl.ds(replica * ticks, ticks)], hs.at[slot])
        fetch(w_hbm.at[replica, 0], ws.at[slot, 0])
        fetch(x_hbm.at[pl.ds(replica * ticks, ticks)], xs.at[slot])
    fetch(l_hbm.at[pl.ds((1 - parity) * (ticks - 1), ticks - 1)], loss)
    for slot, gh_ref, gx_ref in ((0, gh0, gx0), (1, gh1, gx1)):
        for copy in copies[5 * slot : 5 * slot + 5]:
            copy.wait()
        gh_ref[...], gx_ref[...] = step(
            gs[slot][...], xs.at[slot, 0], hs.at[slot, 0], ws.at[slot], pads.at[0], pads.at[1], extent
        )
    copies[-1].wait()

    @pl.when(jnp.logical_not(at_end))
    def _():
        loss[...] = jnp.zeros_like(loss)


def middle_kernel(extent, slot, tick, x_ref, h_ref, w_ref, g_ref, *refs):
    pads = refs[-1]
    g = g_ref[...]
    if slot == 1:
        loss_ref, gh_ref, gx_ref, used_ref = refs[:-1]
        g = (g.astype(F32) + loss_ref[tick - 1].astype(F32)).astype(BF16)
        used_ref[...] = g
    else:
        gh_ref, gx_ref = refs[:-1]
    gh_ref[...], gx_ref[...] = step(
        g,
        x_ref.at[slot, tick],
        h_ref.at[slot, tick],
        w_ref.at[slot],
        pads.at[0],
        pads.at[1],
        extent,
    )


def sums_kernel(extent, ticks, x_ref, h_ref, *refs):
    grads_h, grads = refs[:ticks], refs[ticks : 2 * ticks]
    out_ref, pads = refs[2 * ticks :]
    for pair, (act_ref, sides) in enumerate(((x_ref, grads_h), (h_ref, grads))):
        for n in range(ticks):
            fill_shifts(pads.at[pair, n], sides[n][...], extent)
        acts = [act_ref.at[0, n] for n in range(ticks)]
        total = kernel_sums(acts, [pads.at[pair, n] for n in range(ticks)], extent)
        for row, value in pieces(total, pair):
            out_ref[row : row + PIECE, :] = value.astype(BF16)


def last_kernel(extent, ticks, x_ref, h_ref, w_ref, g_ref, loss_ref, gx0_ref, sums0_ref, *refs):
    early = ticks - 1
    grads_h, grads = refs[:early], refs[early : 2 * early]
    edge_ref, out_ref, pads = refs[2 * early :]
    parity = lax.axis_index("section") & 1
    replica = 1 - parity
    g = (g_ref[...].astype(F32) + loss_ref[early - 1].astype(F32)).astype(BF16)
    _, grad_x = step(
        g,
        x_ref.at[1, early],
        h_ref.at[1, early],
        w_ref.at[1],
        pads.at[1, early],
        pads.at[0, early],
        extent,
    )
    edge_ref[replica] = grad_x
    edge_ref[parity] = gx0_ref[...]
    rows_each = out_ref.shape[2]
    for part in range(out_ref.shape[0]):
        out_ref[part, parity] = sums0_ref[part * rows_each : (part + 1) * rows_each, :]
    for pair, (act_ref, sides) in enumerate(((x_ref, grads_h), (h_ref, grads))):
        for n in range(early):
            fill_shifts(pads.at[pair, n], sides[n][...], extent)
        acts = [act_ref.at[1, n] for n in range(ticks)]
        total = kernel_sums(acts, [pads.at[pair, n] for n in range(ticks)], extent)
        for row, value in pieces(total, pair):
            part, inner = row // rows_each, row % rows_each
            out_ref[part, replica, inner : inner + PIECE, :] = value.astype(BF16)


def call(body, steps, in_specs, out_shape, scratch, args):
    cells, channels = args[0].shape[-2:]
    return pl.pallas_call(
        body,
        in_specs=in_specs,
        out_specs=[vmem()] * len(out_shape),
        out_shape=out_shape,
        scratch_shapes=scratch,
        compiler_params=PARAMS,
        cost_estimate=pl.CostEstimate(
            flops=4 * steps * cells * TAPS * channels * channels,
            bytes_accessed=1000000,
            transcendentals=0,
        ),
    )(*args)


def vmem():
    return pl.BlockSpec(memory_space=pltpu.VMEM)


def in_hbm():
    return pl.BlockSpec(memory_space=pltpu.HBM)


def exchange(value, offset):
    total = lax.axis_size("section")
    pairs = []
    for low in range(offset, total - 1, 2):
        pairs += [(low, low + 1), (low + 1, low)]
    return lax.ppermute(value, "section", pairs)


def on_device(factors, saved_x, saved_h, kernels, grad_in, loss_grads):
    return whole(factors, saved_x, saved_h, kernels, grad_in, loss_grads)


def whole(factors, saved_x, saved_h, kernels, grad_in, loss_grads):
    ticks = saved_x.shape[1]
    extent, channels = saved_x.shape[4], saved_x.shape[6]
    cells = extent * extent
    sections = lax.axis_size("section")
    outer, inner = factors
    rows = 2 * TAPS * channels
    field = (cells, channels)

    def shape(*lead, tail=field):
        return jax.ShapeDtypeStruct((*lead, *tail), BF16)

    def pads(*lead):
        return pltpu.VMEM((*lead, 3, cells + 2 * extent, channels), BF16)

    xs, hs, ws, loss, g0, g1, gh0, gh1, out0, out1 = call(
        functools.partial(first_kernel, extent, ticks),
        2,
        [in_hbm()] * 5,
        [
            shape(2, ticks),
            shape(2, ticks),
            shape(*kernels.shape[1:-2], tail=(channels, channels)),
            shape(ticks - 1),
            *[shape()] * 6,
        ],
        [pads(2), pltpu.SemaphoreType.DMA((11,))],
        [
            pltpu.with_memory_space_constraint(value, pltpu.HBM)
            for value in (
                saved_x.reshape(-1, *field),
                saved_h.reshape(-1, *field),
                kernels[0],
                grad_in.reshape(-1, *field),
                loss_grads.reshape(-1, *field),
            )
        ],
    )
    g, gh = [[g0], [g1]], [[gh0], [gh1]]
    for tick in range(1, ticks):
        far = exchange(out0, 1)
        near = exchange(out1, 0)
        gh0, out0 = call(
            functools.partial(middle_kernel, extent, 0, tick),
            1,
            [vmem()] * 4,
            [shape(), shape()],
            [pads(2)],
            (xs, hs, ws, near),
        )
        g[0].append(near)
        gh[0].append(gh0)
        if tick < ticks - 1:
            gh1, out1, g1 = call(
                functools.partial(middle_kernel, extent, 1, tick),
                1,
                [vmem()] * 5,
                [shape(), shape(), shape()],
                [pads(2)],
                (xs, hs, ws, far, loss),
            )
            g[1].append(g1)
            gh[1].append(gh1)
    (sums0,) = call(
        functools.partial(sums_kernel, extent, ticks),
        ticks,
        [vmem()] * (2 + 2 * ticks),
        [shape(tail=(rows, channels))],
        [pads(2, ticks)],
        (xs, hs, *gh[0], *g[0]),
    )
    edge, both = call(
        functools.partial(last_kernel, extent, ticks),
        1 + ticks,
        [vmem()] * (7 + 2 * (ticks - 1)),
        [shape(2), shape(outer, 2, rows // outer, tail=(channels,))],
        [pads(2, ticks)],
        (xs, hs, ws, far, loss, out0, sums0, *gh[1], *g[1]),
    )
    edge_grads = edge.reshape(2, 1, 1, extent, extent, channels)

    across = [[i * inner + j for i in range(outer)] for j in range(inner)]
    along = [[i * inner + j for j in range(inner)] for i in range(outer)]

    def total(value):
        parts = [value[n].astype(F32) for n in range(value.shape[0])]
        return functools.reduce(lambda a, b: a + b, parts)

    def spread(value, groups):
        return lax.all_to_all(value, "dp", 0, 0, axis_index_groups=groups, tiled=True)

    both = spread(both, across)

    def finish(replica):
        value = total(both[:, replica]).astype(BF16)
        value = value.reshape(inner, rows // outer // inner, channels)
        value = spread(value, along)
        return total(value)

    other = finish(1).astype(BF16)
    other = lax.ppermute(other, "section", [(i, sections - 1 - i) for i in range(sections)])
    mine = finish(0)
    kernel_grads = ((mine + other.astype(F32)) * (1.0 / float(cells)))[None]
    return (kernel_grads, edge_grads)


def solution(mesh):
    shards = mesh.shape["dp"]
    outer = next(f for f in (4, 2, 1) if shards % f == 0)
    return jax.shard_map(
        functools.partial(on_device, (outer, shards // outer)),
        mesh=mesh,
        in_specs=(
            P(None, None, "section", "dp", None, None, None),
            P(None, None, "section", "dp", None, None, None),
            P("section", None, None, None, None, None),
            P(None, "section", "dp", None, None, None),
            P(None, None, "dp", None, None, None),
        ),
        out_specs=(P("section", "dp", None), P(None, "section", "dp", None, None, None)),
        check_vma=False,
    )
```

time: 277 us -> 81.5 us (0.29)
  the two profiles are of different devices: /device:TPU:6 before, /device:TPU:39 now
where the time goes in v2:
time: 81.5 us; the launch traced here: 81.1 us
  starting transfers between devices  43.1 us (53%)
  blocking collectives  25.5 us (31%)
  Pallas kernels  7.61 us (9%)
  waiting for transfers between devices  2.73 us (3%)
  other arithmetic  1.5 us (2%)
    all_to_all x2, blocking collectives, spread(): lax.all_to_all(value, 'dp', 0, 0, axis_index_groups=groups, tiled=True)  25.5 us
    ppermute x4, starting transfers between devices, exchange(): return lax.ppermute(value, 'section', pairs)  22.7 us
    ppermute x1, starting transfers between devices, whole(): lax.ppermute(other, 'section', [(i, sections - 1 - i) for i in range(sect...  15.9 us
    pallas_call x6, Pallas kernels, call(): pl.pallas_call(body, in_specs=in_specs, out_specs=[vmem()] * len(out_shap...  7.61 us
    all_to_all x1, starting transfers between devices, spread(): lax.all_to_all(value, 'dp', 0, 0, axis_index_groups=groups, tiled=True)  4.4 us
    ppermute x1, waiting for transfers between devices, whole(): lax.ppermute(other, 'section', [(i, sections - 1 - i) for i in range(sect...  1.85 us
  transfers between devices with their start and end apart: 6, of which 3 were waited for; matrix products, arithmetic and copies ran while one was open for 0% of the time, Pallas kernels for 4%

profile of v2, /device:TPU:39, one launch (start us, length us, event | category | flops | bytes accessed | tf_op | source)
XLA Modules:
  0.0 81.1 jit_solution(3348209508729468746)
XLA Ops:
  0.6 3.0 %shard_map.68 = (bf16[2,3,256,128]{3,2,1,0:T(8,128)(2,1)S(1)}, bf16[2,3,256,128]{3,2,1,0:T(8,128)(2,1)S(1)}, bf16[2,2,9,128,128]{4,3,2,1,0:T(8,128)(2,1)S(1)}, b...) custom-call(bf16[6,256,128]{2,1,0:T(8,128)(2,1)} %bitcast.22, ...), custom_call_target="tpu_custom_call" | custom-call | flops 301989888 | bytes 1000000 | tf_op jit(solution)/shard_map/pallas_call | solution.py:175
  3.6 9.3 %collective-permute-start.2 = (bf16[256,128]{1,0:T(8,128)(2,1)S(1)}, bf16[256,128]{1,0:T(8,128)(2,1)S(1)}, u32[]{:S(2)}, u32[]{:S(2)}) collective-permute-start(bf16[256,128]{1,0:T(8,128)(2,1)S(1)} %get-tuple-element.27), channel_id=1, source_target_pairs={{16,32},{32,16},{48,64},{64,48},{80,96},{96,80},{112,128},{128,112... | collective-permute-start | bytes 196616 | tf_op jit(solution)/shard_map/ppermute | solution.py:203
  12.9 1.9 %collective-permute-start = (bf16[256,128]{1,0:T(8,128)(2,1)S(1)}, bf16[256,128]{1,0:T(8,128)(2,1)S(1)}, u32[]{:S(2)}, u32[]{:S(2)}) collective-permute-start(bf16[256,128]{1,0:T(8,128)(2,1)S(1)} %get-tuple-element.24), channel_id=1, source_target_pairs={{0,16},{16,0},{32,48},{48,32},{64,80},{80,64},{96,112},{112,96},{1... | collective-permute-start | bytes 196616 | tf_op jit(solution)/shard_map/ppermute | solution.py:203
  14.8 0.4 collective-permute-done.2.g_ref
  15.2 0.8 shard_map.70
  16.0 2.0 %collective-permute-start.3 = (bf16[256,128]{1,0:T(8,128)(2,1)S(1)}, bf16[256,128]{1,0:T(8,128)(2,1)S(1)}, u32[]{:S(2)}, u32[]{:S(2)}) collective-permute-start(bf16[256,128]{1,0:T(8,128)(2,1)S(1)} %get-tuple-element.28), channel_id=1, source_target_pairs={{0,16},{16,0},{32,48},{48,32},{64,80},{80,64},{96,112},{112,96},{1... | collective-permute-start | bytes 196616 | tf_op jit(solution)/shard_map/ppermute | solution.py:203
  18.0 0.0 collective-permute-done.g_ref.refs_4_
  18.1 0.8 shard_map.69
  18.8 9.5 %collective-permute-start.1 = (bf16[256,128]{1,0:T(8,128)(2,1)S(1)}, bf16[256,128]{1,0:T(8,128)(2,1)S(1)}, u32[]{:S(2)}, u32[]{:S(2)}) collective-permute-start(bf16[256,128]{1,0:T(8,128)(2,1)S(1)} %get-tuple-element.25), channel_id=1, source_target_pairs={{16,32},{32,16},{48,64},{64,48},{80,96},{96,80},{112,128},{128,112... | collective-permute-start | bytes 196616 | tf_op jit(solution)/shard_map/ppermute | solution.py:203
  28.3 0.0 collective-permute-done.3.g_ref.refs_5_
  28.3 0.8 shard_map.71
  29.1 0.8 %shard_map.72.sums0_ref = bf16[2304,128]{1,0:T(8,128)(2,1)S(1)} custom-call(bf16[2,3,256,128]{3,2,1,0:T(8,128)(2,1)S(1)} %get-tuple-element.21.x_ref, bf16[2,3,256,128]{3,2,1,0:T(8,128)(2,1)S(1)} %get-tuple-element.22.h_ref, bf16[256,128]{1,0:T(8,128)(2,1)S(1)} %get-tuple-element.30.refs_0_, bf16[256,128]{1,0:T(8,128)(2,1)S(1)} %get-tuple-element.31.refs_1_, ...), custom_call_target="tpu_custom_call" | custom-call | flops 452984832 | bytes 1000000 | tf_op jit(solution)/shard_map/pallas_call | solution.py:175
  29.9 0.5 collective-permute-done.1.g_ref
  30.4 1.5 %shard_map.73 = (bf16[2,256,128]{2,1,0:T(8,128)(2,1)}, bf16[4,2,576,128]{3,2,1,0:T(8,128)(2,1)S(1)}) custom-call(bf16[2,3,256,128]{3,2,1,0:T(8,128)(2,1)S(1)} %get-tuple-element.21.x_ref, bf16[2,3,256,128]{3,2,1,0:T(8,128)(2,1)S(1)} %get-tuple-element.22.h_ref, bf16[2,2,9,128,128]{4,3,2,1,0:T(8,128)(2,1)S(1)} %get-tuple-element.23.w_ref, ...), custom_call_target="tpu_custom_call" | custom-call | flops 603979776 | bytes 1000000 | tf_op jit(solution)/shard_map/pallas_call | solution.py:175
  31.9 15.8 %all_to_all.15 = bf16[4,2,576,128]{3,2,1,0:T(8,128)(2,1)S(1)} all-to-all(bf16[4,2,576,128]{3,2,1,0:T(8,128)(2,1)S(1)} %get-tuple-element.38), channel_id=1, replica_groups={{0,4,8,12},{1,5,9,13},{2,6,10,14},{3,7,11,15},{16,20,24,28},{17,21,25,2..., dimensions={0} | all-to-all | bytes 2359296 | tf_op jit(solution)/shard_map/all_to_all | solution.py:299
  47.8 0.8 %add_convert_fusion.1 = (bf16[1,1,576,128]{3,2,1,0:T(8,128)(2,1)}, bf16[1,1,576,128]{3,2,1,0:T(8,128)(2,1)S(1)}) fusion(bf16[4,2,576,128]{3,2,1,0:T(8,128)(2,1)S(1)} %all_to_all.15), kind=kLoop, calls=%fused_computation.1 | loop fusion | flops 1179648 | bytes 1474560 | tf_op jit(solution)/shard_map/convert.2
  48.6 9.7 %all_to_all.16 = bf16[4,144,128]{2,1,0:T(8,128)(2,1)S(1)} all-to-all(bf16[4,144,128]{2,1,0:T(8,128)(2,1)S(1)} %bitcast.21), channel_id=1, replica_groups={{0,1,2,3},{4,5,6,7},{8,9,10,11},{12,13,14,15},{16,17,18,19},{20,21,22,2..., dimensions={0} | all-to-all | bytes 294912 | tf_op jit(solution)/shard_map/all_to_all | solution.py:299
  58.2 4.4 %all-to-all-start.1 = ((bf16[4,144,128]{2,1,0:T(8,128)(2,1)}), bf16[4,144,128]{2,1,0:T(8,128)(2,1)S(1)}, u32[]{:S(2)}, u32[]{:S(2)}) async-start(bf16[4,144,128]{2,1,0:T(8,128)(2,1)} %bitcast.5), calls=%async_computation.1 | async-start | bytes 294912 | tf_op jit(solution)/shard_map/all_to_all | solution.py:299
  62.6 15.9 %collective-permute-start.4 = (bf16[144,128]{1,0:T(8,128)(2,1)S(1)}, bf16[144,128]{1,0:T(8,128)(2,1)S(1)}, u32[]{:S(2)}, u32[]{:S(2)}) collective-permute-start(bf16[144,128]{1,0:T(8,128)(2,1)S(1)} %fusion.2), channel_id=1, source_target_pairs={{0,496},{16,480},{32,464},{48,448},{64,432},{80,416},{96,400},{112... | collective-permute-start | bytes 110600 | tf_op jit(solution)/shard_map/ppermute | solution.py:310
  78.6 0.0 all-to-all-done.1
  78.6 1.9 %collective-permute-done.4 = bf16[144,128]{1,0:T(8,128)(2,1)S(1)} collective-permute-done((bf16[144,128]{1,0:T(8,128)(2,1)S(1)}, bf16[144,128]{1,0:T(8,128)(2,1)S(1)}, u32[]{:S(2)}, u32[]{:S(2)}) %collective-permute-start.4) | collective-permute-done | bytes 36896 | tf_op jit(solution)/shard_map/ppermute | solution.py:310
  80.5 0.7 fusion.1
  (1 shorter events, 0.0 us)
Async XLA Ops:
  3.6 11.6 %collective-permute-start.2 = (bf16[256,128]{1,0:T(8,128)(2,1)S(1)}, bf16[256,128]{1,0:T(8,128)(2,1)S(1)}, u32[]{:S(2)}, u32[]{:S(2)}) collective-permute-start(bf16[256,128]{1,0:T(8,128)(2,1)S(1)} %get-tuple-element.27), channel_id=1, source_target_pairs={{16,32},{32,16},{48,64},{64,48},{80,96},{96,80},{112,128},{128,112... | collective-permute-start | bytes 196616 | tf_op jit(solution)/shard_map/ppermute | solution.py:203
  12.9 5.1 %collective-permute-start = (bf16[256,128]{1,0:T(8,128)(2,1)S(1)}, bf16[256,128]{1,0:T(8,128)(2,1)S(1)}, u32[]{:S(2)}, u32[]{:S(2)}) collective-permute-start(bf16[256,128]{1,0:T(8,128)(2,1)S(1)} %get-tuple-element.24), channel_id=1, source_target_pairs={{0,16},{16,0},{32,48},{48,32},{64,80},{80,64},{96,112},{112,96},{1... | collective-permute-start | bytes 196616 | tf_op jit(solution)/shard_map/ppermute | solution.py:203
  16.0 12.3 %collective-permute-start.3 = (bf16[256,128]{1,0:T(8,128)(2,1)S(1)}, bf16[256,128]{1,0:T(8,128)(2,1)S(1)}, u32[]{:S(2)}, u32[]{:S(2)}) collective-permute-start(bf16[256,128]{1,0:T(8,128)(2,1)S(1)} %get-tuple-element.28), channel_id=1, source_target_pairs={{0,16},{16,0},{32,48},{48,32},{64,80},{80,64},{96,112},{112,96},{1... | collective-permute-start | bytes 196616 | tf_op jit(solution)/shard_map/ppermute | solution.py:203
  18.8 11.6 %collective-permute-start.1 = (bf16[256,128]{1,0:T(8,128)(2,1)S(1)}, bf16[256,128]{1,0:T(8,128)(2,1)S(1)}, u32[]{:S(2)}, u32[]{:S(2)}) collective-permute-start(bf16[256,128]{1,0:T(8,128)(2,1)S(1)} %get-tuple-element.25), channel_id=1, source_target_pairs={{16,32},{32,16},{48,64},{64,48},{80,96},{96,80},{112,128},{128,112... | collective-permute-start | bytes 196616 | tf_op jit(solution)/shard_map/ppermute | solution.py:203
  58.2 20.4 %all-to-all-start.1 = ((bf16[4,144,128]{2,1,0:T(8,128)(2,1)}), bf16[4,144,128]{2,1,0:T(8,128)(2,1)S(1)}, u32[]{:S(2)}, u32[]{:S(2)}) async-start(bf16[4,144,128]{2,1,0:T(8,128)(2,1)} %bitcast.5), calls=%async_computation.1 | async-start | bytes 294912 | tf_op jit(solution)/shard_map/all_to_all | solution.py:299
  62.6 17.8 %collective-permute-start.4 = (bf16[144,128]{1,0:T(8,128)(2,1)S(1)}, bf16[144,128]{1,0:T(8,128)(2,1)S(1)}, u32[]{:S(2)}, u32[]{:S(2)}) collective-permute-start(bf16[144,128]{1,0:T(8,128)(2,1)S(1)} %fusion.2), channel_id=1, source_target_pairs={{0,496},{16,480},{32,464},{48,448},{64,432},{80,416},{96,400},{112... | collective-permute-start | bytes 110600 | tf_op jit(solution)/shard_map/ppermute | solution.py:310

commit v3 on v2

--- a/solution.py
+++ b/solution.py
@@ -9,7 +9,7 @@
 
 
 TAPS = 9
-PIECE = 64
+PIECE = 16
 PARAMS = pltpu.CompilerParams(vmem_limit_bytes=16 << 20)
 BF16, F32 = jnp.bfloat16, jnp.float32
 
@@ -139,11 +139,12 @@
             out_ref[row : row + PIECE, :] = value.astype(BF16)
 
 
-def last_kernel(extent, ticks, x_ref, h_ref, w_ref, g_ref, loss_ref, gx0_ref, sums0_ref, *refs):
+def last_kernel(extent, ticks, parts, x_ref, h_ref, w_ref, g_ref, loss_ref, gx0_ref, sums0_ref, *refs):
     early = ticks - 1
     grads_h, grads = refs[:early], refs[early : 2 * early]
     edge_ref, out_ref, pads = refs[2 * early :]
-    parity = lax.axis_index("section") & 1
+    position = lax.axis_index("section")
+    parity = position & 1
     replica = 1 - parity
     g = (g_ref[...].astype(F32) + loss_ref[early - 1].astype(F32)).astype(BF16)
     _, grad_x = step(
@@ -157,17 +158,25 @@
     )
     edge_ref[replica] = grad_x
     edge_ref[parity] = gx0_ref[...]
-    rows_each = out_ref.shape[2]
-    for part in range(out_ref.shape[0]):
-        out_ref[part, parity] = sums0_ref[part * rows_each : (part + 1) * rows_each, :]
+    members, _, later, rows_each, _ = out_ref.shape
+    upper = (position >= lax.axis_size("section") // 2).astype(jnp.int32)
+    half0, half1 = (parity + upper) & 1, (replica + upper) & 1
+
+    def put(row, half, value):
+        shard, inner = row // rows_each, row % rows_each
+        block, pair_at = shard // (2 * later), shard % (2 * later)
+        member = block * (members // parts) + pair_at % 2
+        out_ref[member, half, pair_at // 2, inner : inner + value.shape[0], :] = value
+
+    for row in range(0, sums0_ref.shape[0], rows_each):
+        put(row, half0, sums0_ref[row : row + rows_each, :])
     for pair, (act_ref, sides) in enumerate(((x_ref, grads_h), (h_ref, grads))):
         for n in range(early):
             fill_shifts(pads.at[pair, n], sides[n][...], extent)
         acts = [act_ref.at[1, n] for n in range(ticks)]
         total = kernel_sums(acts, [pads.at[pair, n] for n in range(ticks)], extent)
         for row, value in pieces(total, pair):
-            part, inner = row // rows_each, row % rows_each
-            out_ref[part, replica, inner : inner + PIECE, :] = value.astype(BF16)
+            put(row, half1, value.astype(BF16))
 
 
 def call(body, steps, in_specs, out_shape, scratch, args):
@@ -213,6 +222,7 @@
     cells = extent * extent
     sections = lax.axis_size("section")
     outer, inner = factors
+    later, shards = inner // 2, outer * inner
     rows = 2 * TAPS * channels
     field = (cells, channels)
 
@@ -279,37 +289,43 @@
         (xs, hs, *gh[0], *g[0]),
     )
     edge, both = call(
-        functools.partial(last_kernel, extent, ticks),
+        functools.partial(last_kernel, extent, ticks, outer),
         1 + ticks,
         [vmem()] * (7 + 2 * (ticks - 1)),
-        [shape(2), shape(outer, 2, rows // outer, tail=(channels,))],
+        [shape(2), shape(2 * outer, 2, later, rows // shards, tail=(channels,))],
         [pads(2, ticks)],
         (xs, hs, ws, far, loss, out0, sums0, *gh[1], *g[1]),
     )
     edge_grads = edge.reshape(2, 1, 1, extent, extent, channels)
 
-    across = [[i * inner + j for i in range(outer)] for j in range(inner)]
-    along = [[i * inner + j for j in range(inner)] for i in range(outer)]
+    def shard(block, far, near):
+        return (block * later + far) * 2 + near
+
+    first_groups = [
+        [shard(block, far, near) for block in range(outer) for near in range(2)]
+        for far in range(later)
+    ]
+    second_groups = [
+        [
+            section * shards + shard(block, far, near)
+            for section in (low, sections - 1 - low)
+            for far in range(later)
+        ]
+        for low in range(sections // 2)
+        for block in range(outer)
+        for near in range(2)
+    ]
 
     def total(value):
         parts = [value[n].astype(F32) for n in range(value.shape[0])]
         return functools.reduce(lambda a, b: a + b, parts)
 
-    def spread(value, groups):
-        return lax.all_to_all(value, "dp", 0, 0, axis_index_groups=groups, tiled=True)
-
-    both = spread(both, across)
-
-    def finish(replica):
-        value = total(both[:, replica]).astype(BF16)
-        value = value.reshape(inner, rows // outer // inner, channels)
-        value = spread(value, along)
-        return total(value)
-
-    other = finish(1).astype(BF16)
-    other = lax.ppermute(other, "section", [(i, sections - 1 - i) for i in range(sections)])
-    mine = finish(0)
-    kernel_grads = ((mine + other.astype(F32)) * (1.0 / float(cells)))[None]
+    both = lax.all_to_all(both, "dp", 0, 0, axis_index_groups=first_groups, tiled=True)
+    both = total(both).astype(BF16).reshape(2 * later, rows // shards, channels)
+    both = lax.all_to_all(
+        both, ("section", "dp"), 0, 0, axis_index_groups=second_groups, tiled=True
+    )
+    kernel_grads = (total(both) * (1.0 / float(cells)))[None]
     return (kernel_grads, edge_grads)
 
 

time: 81.5 us -> 79.7 us (0.978)
  the two profiles are of different devices: /device:TPU:39 before, /device:TPU:7 now
where the time goes in v3:
time: 79.7 us; the launch traced here: 79.4 us
  blocking collectives  46.6 us (58%)
  starting transfers between devices  22.5 us (28%)
  Pallas kernels  7.61 us (10%)
  waiting for transfers between devices  1.27 us (2%)
  other arithmetic  0.81 us (1%)
    all_to_all x1, blocking collectives, whole(): lax.all_to_all(both, ('section', 'dp'), 0, 0, axis_index_groups=second_gr...  28.8 us
    ppermute x4, starting transfers between devices, exchange(): return lax.ppermute(value, 'section', pairs)  22.5 us
    all_to_all x1, blocking collectives, whole(): lax.all_to_all(both, 'dp', 0, 0, axis_index_groups=first_groups, tiled=True)  17.8 us
    pallas_call x6, Pallas kernels, call(): pl.pallas_call(body, in_specs=in_specs, out_specs=[vmem()] * len(out_shap...  7.61 us
  transfers between devices with their start and end apart: 4, of which 2 were waited for; matrix products, arithmetic and copies ran while one was open for 0% of the time, Pallas kernels for 4%

profile of v3, /device:TPU:7, one launch (start us, length us, event | category | flops | bytes accessed | tf_op | source)
XLA Modules:
  0.0 79.4 jit_solution(14049091498496251762)
XLA Ops:
  0.6 3.0 %shard_map.68 = (bf16[2,3,256,128]{3,2,1,0:T(8,128)(2,1)S(1)}, bf16[2,3,256,128]{3,2,1,0:T(8,128)(2,1)S(1)}, bf16[2,2,9,128,128]{4,3,2,1,0:T(8,128)(2,1)S(1)}, b...) custom-call(bf16[6,256,128]{2,1,0:T(8,128)(2,1)} %bitcast.11, ...), custom_call_target="tpu_custom_call" | custom-call | flops 301989888 | bytes 1000000 | tf_op jit(solution)/shard_map/pallas_call | solution.py:184
  3.6 9.3 %collective-permute-start.2 = (bf16[256,128]{1,0:T(8,128)(2,1)S(1)}, bf16[256,128]{1,0:T(8,128)(2,1)S(1)}, u32[]{:S(2)}, u32[]{:S(2)}) collective-permute-start(bf16[256,128]{1,0:T(8,128)(2,1)S(1)} %get-tuple-element.27), channel_id=1, source_target_pairs={{16,32},{32,16},{48,64},{64,48},{80,96},{96,80},{112,128},{128,112... | collective-permute-start | bytes 196616 | tf_op jit(solution)/shard_map/ppermute | solution.py:212
  12.9 1.9 %collective-permute-start = (bf16[256,128]{1,0:T(8,128)(2,1)S(1)}, bf16[256,128]{1,0:T(8,128)(2,1)S(1)}, u32[]{:S(2)}, u32[]{:S(2)}) collective-permute-start(bf16[256,128]{1,0:T(8,128)(2,1)S(1)} %get-tuple-element.24), channel_id=1, source_target_pairs={{0,16},{16,0},{32,48},{48,32},{64,80},{80,64},{96,112},{112,96},{1... | collective-permute-start | bytes 196616 | tf_op jit(solution)/shard_map/ppermute | solution.py:212
  14.8 0.4 collective-permute-done.2.g_ref
  15.2 0.8 shard_map.70
  16.0 2.1 %collective-permute-start.3 = (bf16[256,128]{1,0:T(8,128)(2,1)S(1)}, bf16[256,128]{1,0:T(8,128)(2,1)S(1)}, u32[]{:S(2)}, u32[]{:S(2)}) collective-permute-start(bf16[256,128]{1,0:T(8,128)(2,1)S(1)} %get-tuple-element.28), channel_id=1, source_target_pairs={{0,16},{16,0},{32,48},{48,32},{64,80},{80,64},{96,112},{112,96},{1... | collective-permute-start | bytes 196616 | tf_op jit(solution)/shard_map/ppermute | solution.py:212
  18.0 0.0 collective-permute-done.g_ref.refs_4_
  18.1 0.8 shard_map.69
  18.8 9.2 %collective-permute-start.1 = (bf16[256,128]{1,0:T(8,128)(2,1)S(1)}, bf16[256,128]{1,0:T(8,128)(2,1)S(1)}, u32[]{:S(2)}, u32[]{:S(2)}) collective-permute-start(bf16[256,128]{1,0:T(8,128)(2,1)S(1)} %get-tuple-element.25), channel_id=1, source_target_pairs={{16,32},{32,16},{48,64},{64,48},{80,96},{96,80},{112,128},{128,112... | collective-permute-start | bytes 196616 | tf_op jit(solution)/shard_map/ppermute | solution.py:212
  28.0 0.0 collective-permute-done.3.g_ref.refs_5_
  28.1 0.8 shard_map.71
  28.8 0.8 %shard_map.72.sums0_ref = bf16[2304,128]{1,0:T(8,128)(2,1)S(1)} custom-call(bf16[2,3,256,128]{3,2,1,0:T(8,128)(2,1)S(1)} %get-tuple-element.21.x_ref, bf16[2,3,256,128]{3,2,1,0:T(8,128)(2,1)S(1)} %get-tuple-element.22.h_ref, bf16[256,128]{1,0:T(8,128)(2,1)S(1)} %get-tuple-element.30.refs_0_, bf16[256,128]{1,0:T(8,128)(2,1)S(1)} %get-tuple-element.31.refs_1_, ...), custom_call_target="tpu_custom_call" | custom-call | flops 452984832 | bytes 1000000 | tf_op jit(solution)/shard_map/pallas_call | solution.py:184
  29.7 0.9 %collective-permute-done.1.g_ref = bf16[256,128]{1,0:T(8,128)(2,1)S(1)} collective-permute-done((bf16[256,128]{1,0:T(8,128)(2,1)S(1)}, bf16[256,128]{1,0:T(8,128)(2,1)S(1)}, u32[]{:S(2)}, u32[]{:S(2)}) %collective-permute-start.1) | collective-permute-done | bytes 65568 | tf_op jit(solution)/shard_map/ppermute | solution.py:212
  30.6 1.5 %shard_map.73 = (bf16[2,256,128]{2,1,0:T(8,128)(2,1)}, bf16[8,2,2,144,128]{4,3,2,1,0:T(8,128)(2,1)S(1)}) custom-call(bf16[2,3,256,128]{3,2,1,0:T(8,128)(2,1)S(1)} %get-tuple-element.21.x_ref, bf16[2,3,256,128]{3,2,1,0:T(8,128)(2,1)S(1)} %get-tuple-element.22.h_ref, bf16[2,2,9,128,128]{4,3,2,1,0:T(8,128)(2,1)S(1)} %get-tuple-element.23.w_ref, ...), custom_call_target="tpu_custom_call" | custom-call | flops 603979776 | bytes 1000000 | tf_op jit(solution)/shard_map/pallas_call | solution.py:184
  32.0 17.8 %all_to_all.10 = bf16[8,2,2,144,128]{4,3,2,1,0:T(8,128)(2,1)S(1)} all-to-all(bf16[8,2,2,144,128]{4,3,2,1,0:T(8,128)(2,1)S(1)} %get-tuple-element.38), channel_id=1, replica_groups={{0,1,4,5,8,9,12,13},{2,3,6,7,10,11,14,15},{16,17,20,21,24,25,28,29},{18..., dimensions={0} | all-to-all | bytes 2359296 | tf_op jit(solution)/shard_map/all_to_all | solution.py:323
  49.8 0.2 add_convert_fusion
  50.0 28.8 %all_to_all.11 = bf16[4,144,128]{2,1,0:T(8,128)(2,1)S(1)} all-to-all(bf16[4,144,128]{2,1,0:T(8,128)(2,1)S(1)} %bitcast.10), channel_id=1, replica_groups={{0,2,496,498},{1,3,497,499},{4,6,500,502},{5,7,501,503},{8,10,504,506},..., dimensions={0} | all-to-all | bytes 294912 | tf_op jit(solution)/shard_map/all_to_all | solution.py:325
  78.8 0.7 add_multiply_fusion
Async XLA Ops:
  3.6 11.6 %collective-permute-start.2 = (bf16[256,128]{1,0:T(8,128)(2,1)S(1)}, bf16[256,128]{1,0:T(8,128)(2,1)S(1)}, u32[]{:S(2)}, u32[]{:S(2)}) collective-permute-start(bf16[256,128]{1,0:T(8,128)(2,1)S(1)} %get-tuple-element.27), channel_id=1, source_target_pairs={{16,32},{32,16},{48,64},{64,48},{80,96},{96,80},{112,128},{128,112... | collective-permute-start | bytes 196616 | tf_op jit(solution)/shard_map/ppermute | solution.py:212
  12.9 5.2 %collective-permute-start = (bf16[256,128]{1,0:T(8,128)(2,1)S(1)}, bf16[256,128]{1,0:T(8,128)(2,1)S(1)}, u32[]{:S(2)}, u32[]{:S(2)}) collective-permute-start(bf16[256,128]{1,0:T(8,128)(2,1)S(1)} %get-tuple-element.24), channel_id=1, source_target_pairs={{0,16},{16,0},{32,48},{48,32},{64,80},{80,64},{96,112},{112,96},{1... | collective-permute-start | bytes 196616 | tf_op jit(solution)/shard_map/ppermute | solution.py:212
  16.0 12.1 %collective-permute-start.3 = (bf16[256,128]{1,0:T(8,128)(2,1)S(1)}, bf16[256,128]{1,0:T(8,128)(2,1)S(1)}, u32[]{:S(2)}, u32[]{:S(2)}) collective-permute-start(bf16[256,128]{1,0:T(8,128)(2,1)S(1)} %get-tuple-element.28), channel_id=1, source_target_pairs={{0,16},{16,0},{32,48},{48,32},{64,80},{80,64},{96,112},{112,96},{1... | collective-permute-start | bytes 196616 | tf_op jit(solution)/shard_map/ppermute | solution.py:212
  18.8 11.7 %collective-permute-start.1 = (bf16[256,128]{1,0:T(8,128)(2,1)S(1)}, bf16[256,128]{1,0:T(8,128)(2,1)S(1)}, u32[]{:S(2)}, u32[]{:S(2)}) collective-permute-start(bf16[256,128]{1,0:T(8,128)(2,1)S(1)} %get-tuple-element.25), channel_id=1, source_target_pairs={{16,32},{32,16},{48,64},{64,48},{80,96},{96,80},{112,128},{128,112... | collective-permute-start | bytes 196616 | tf_op jit(solution)/shard_map/ppermute | solution.py:212

commit v4 on v3

--- a/solution.py
+++ b/solution.py
@@ -90,9 +90,14 @@
         replica = parity if slot == 0 else 1 - parity
         fetch(g_hbm.at[replica], gs[slot])
         fetch(w_hbm.at[replica, 1], ws.at[slot, 1])
-        fetch(h_hbm.at[pl.ds(replica * ticks, ticks)], hs.at[slot])
+        fetch(h_hbm.at[replica * ticks], hs.at[slot, 0])
         fetch(w_hbm.at[replica, 0], ws.at[slot, 0])
-        fetch(x_hbm.at[pl.ds(replica * ticks, ticks)], xs.at[slot])
+        fetch(x_hbm.at[replica * ticks], xs.at[slot, 0])
+    for slot in (0, 1):
+        replica = parity if slot == 0 else 1 - parity
+        later = pl.ds(replica * ticks + 1, ticks - 1)
+        fetch(h_hbm.at[later], hs.at[slot, pl.ds(1, ticks - 1)])
+        fetch(x_hbm.at[later], xs.at[slot, pl.ds(1, ticks - 1)])
     fetch(l_hbm.at[pl.ds((1 - parity) * (ticks - 1), ticks - 1)], loss)
     for slot, gh_ref, gx_ref in ((0, gh0, gx0), (1, gh1, gx1)):
         for copy in copies[5 * slot : 5 * slot + 5]:
@@ -100,7 +105,8 @@
         gh_ref[...], gx_ref[...] = step(
             gs[slot][...], xs.at[slot, 0], hs.at[slot, 0], ws.at[slot], pads.at[0], pads.at[1], extent
         )
-    copies[-1].wait()
+    for copy in copies[10:]:
+        copy.wait()
 
     @pl.when(jnp.logical_not(at_end))
     def _():
@@ -127,11 +133,21 @@
     )
 
 
-def sums_kernel(extent, ticks, x_ref, h_ref, *refs):
-    grads_h, grads = refs[:ticks], refs[ticks : 2 * ticks]
-    out_ref, pads = refs[2 * ticks :]
+def even_last_kernel(extent, ticks, x_ref, h_ref, w_ref, g_ref, *refs):
+    early = ticks - 1
+    grads_h, grads = refs[:early], refs[early : 2 * early]
+    gx_ref, out_ref, pads = refs[2 * early :]
+    _, gx_ref[...] = step(
+        g_ref[...],
+        x_ref.at[0, early],
+        h_ref.at[0, early],
+        w_ref.at[0],
+        pads.at[1, early],
+        pads.at[0, early],
+        extent,
+    )
     for pair, (act_ref, sides) in enumerate(((x_ref, grads_h), (h_ref, grads))):
-        for n in range(ticks):
+        for n in range(early):
             fill_shifts(pads.at[pair, n], sides[n][...], extent)
         acts = [act_ref.at[0, n] for n in range(ticks)]
         total = kernel_sums(acts, [pads.at[pair, n] for n in range(ticks)], extent)
@@ -243,7 +259,7 @@
             shape(ticks - 1),
             *[shape()] * 6,
         ],
-        [pads(2), pltpu.SemaphoreType.DMA((11,))],
+        [pads(2), pltpu.SemaphoreType.DMA((15,))],
         [
             pltpu.with_memory_space_constraint(value, pltpu.HBM)
             for value in (
@@ -259,6 +275,8 @@
     for tick in range(1, ticks):
         far = exchange(out0, 1)
         near = exchange(out1, 0)
+        if tick == ticks - 1:
+            break
         gh0, out0 = call(
             functools.partial(middle_kernel, extent, 0, tick),
             1,
@@ -267,26 +285,24 @@
             [pads(2)],
             (xs, hs, ws, near),
         )
-        g[0].append(near)
-        gh[0].append(gh0)
-        if tick < ticks - 1:
-            gh1, out1, g1 = call(
-                functools.partial(middle_kernel, extent, 1, tick),
-                1,
-                [vmem()] * 5,
-                [shape(), shape(), shape()],
-                [pads(2)],
-                (xs, hs, ws, far, loss),
-            )
-            g[1].append(g1)
-            gh[1].append(gh1)
-    (sums0,) = call(
-        functools.partial(sums_kernel, extent, ticks),
-        ticks,
-        [vmem()] * (2 + 2 * ticks),
-        [shape(tail=(rows, channels))],
+        gh1, out1, g1 = call(
+            functools.partial(middle_kernel, extent, 1, tick),
+            1,
+            [vmem()] * 5,
+            [shape(), shape(), shape()],
+            [pads(2)],
+            (xs, hs, ws, far, loss),
+        )
+        for slot, used, made in ((0, near, gh0), (1, g1, gh1)):
+            g[slot].append(used)
+            gh[slot].append(made)
+    out0, sums0 = call(
+        functools.partial(even_last_kernel, extent, ticks),
+        1 + ticks,
+        [vmem()] * (4 + 2 * (ticks - 1)),
+        [shape(), shape(tail=(rows, channels))],
         [pads(2, ticks)],
-        (xs, hs, *gh[0], *g[0]),
+        (xs, hs, ws, near, *gh[0], *g[0]),
     )
     edge, both = call(
         functools.partial(last_kernel, extent, ticks, outer),

time: 79.7 us -> 79.7 us (level)
    pallas_call x6 -> x5, Pallas kernels: 7.61 us -> 7.27 us  [call(): pl.pallas_call(body, in_specs=in_specs, out_specs=[vmem()] * len(out_shap...]
where the time goes in v4:
time: 79.7 us; the launch traced here: 79.4 us
  blocking collectives  46.6 us (58%)
  starting transfers between devices  22.4 us (28%)
  Pallas kernels  7.27 us (9%)
  waiting for transfers between devices  1.55 us (2%)
  other arithmetic  0.81 us (1%)
    all_to_all x1, blocking collectives, whole(): lax.all_to_all(both, ('section', 'dp'), 0, 0, axis_index_groups=second_gr...  28.8 us
    ppermute x4, starting transfers between devices, exchange(): return lax.ppermute(value, 'section', pairs)  22.4 us
    all_to_all x1, blocking collectives, whole(): lax.all_to_all(both, 'dp', 0, 0, axis_index_groups=first_groups, tiled=True)  17.8 us
    pallas_call x5, Pallas kernels, call(): pl.pallas_call(body, in_specs=in_specs, out_specs=[vmem()] * len(out_shap...  7.27 us
  transfers between devices with their start and end apart: 4, of which 2 were waited for; matrix products, arithmetic and copies ran while one was open for 0% of the time, Pallas kernels for 4%

profile of v4, /device:TPU:7, one launch (start us, length us, event | category | flops | bytes accessed | tf_op | source)
XLA Modules:
  0.0 79.4 jit_solution(17603069399988870694)
XLA Ops:
  0.6 2.9 %shard_map.68 = (bf16[2,3,256,128]{3,2,1,0:T(8,128)(2,1)S(1)}, bf16[2,3,256,128]{3,2,1,0:T(8,128)(2,1)S(1)}, bf16[2,2,9,128,128]{4,3,2,1,0:T(8,128)(2,1)S(1)}, b...) custom-call(bf16[6,256,128]{2,1,0:T(8,128)(2,1)} %bitcast.11, ...), custom_call_target="tpu_custom_call" | custom-call | flops 301989888 | bytes 1000000 | tf_op jit(solution)/shard_map/pallas_call | solution.py:200
  3.5 9.3 %collective-permute-start.2 = (bf16[256,128]{1,0:T(8,128)(2,1)S(1)}, bf16[256,128]{1,0:T(8,128)(2,1)S(1)}, u32[]{:S(2)}, u32[]{:S(2)}) collective-permute-start(bf16[256,128]{1,0:T(8,128)(2,1)S(1)} %get-tuple-element.27), channel_id=1, source_target_pairs={{16,32},{32,16},{48,64},{64,48},{80,96},{96,80},{112,128},{128,112... | collective-permute-start | bytes 196616 | tf_op jit(solution)/shard_map/ppermute | solution.py:228
  12.8 1.9 %collective-permute-start = (bf16[256,128]{1,0:T(8,128)(2,1)S(1)}, bf16[256,128]{1,0:T(8,128)(2,1)S(1)}, u32[]{:S(2)}, u32[]{:S(2)}) collective-permute-start(bf16[256,128]{1,0:T(8,128)(2,1)S(1)} %get-tuple-element.24), channel_id=1, source_target_pairs={{0,16},{16,0},{32,48},{48,32},{64,80},{80,64},{96,112},{112,96},{1... | collective-permute-start | bytes 196616 | tf_op jit(solution)/shard_map/ppermute | solution.py:228
  14.7 0.4 collective-permute-done.2.g_ref
  15.1 0.8 shard_map.70
  15.9 2.0 %collective-permute-start.3 = (bf16[256,128]{1,0:T(8,128)(2,1)S(1)}, bf16[256,128]{1,0:T(8,128)(2,1)S(1)}, u32[]{:S(2)}, u32[]{:S(2)}) collective-permute-start(bf16[256,128]{1,0:T(8,128)(2,1)S(1)} %get-tuple-element.28), channel_id=1, source_target_pairs={{0,16},{16,0},{32,48},{48,32},{64,80},{80,64},{96,112},{112,96},{1... | collective-permute-start | bytes 196616 | tf_op jit(solution)/shard_map/ppermute | solution.py:228
  18.0 0.0 collective-permute-done.g_ref.refs_3_
  18.0 0.8 shard_map.69
  18.8 9.2 %collective-permute-start.1 = (bf16[256,128]{1,0:T(8,128)(2,1)S(1)}, bf16[256,128]{1,0:T(8,128)(2,1)S(1)}, u32[]{:S(2)}, u32[]{:S(2)}) collective-permute-start(bf16[256,128]{1,0:T(8,128)(2,1)S(1)} %get-tuple-element.25), channel_id=1, source_target_pairs={{16,32},{32,16},{48,64},{64,48},{80,96},{96,80},{112,128},{128,112... | collective-permute-start | bytes 196616 | tf_op jit(solution)/shard_map/ppermute | solution.py:228
  28.0 0.0 collective-permute-done.3.g_ref
  28.0 1.3 %shard_map.71 = (bf16[256,128]{1,0:T(8,128)(2,1)S(1)}, bf16[2304,128]{1,0:T(8,128)(2,1)S(1)}) custom-call(bf16[2,3,256,128]{3,2,1,0:T(8,128)(2,1)S(1)} %get-tuple-element.21.x_ref, bf16[2,3,256,128]{3,2,1,0:T(8,128)(2,1)S(1)} %get-tuple-element.22.h_ref, bf16[2,2,9,128,128]{4,3,2,1,0:T(8,128)(2,1)S(1)} %get-tuple-element.23.w_ref, ...), custom_call_target="tpu_custom_call" | custom-call | flops 603979776 | bytes 1000000 | tf_op jit(solution)/shard_map/pallas_call | solution.py:200
  29.3 1.2 %collective-permute-done.1.g_ref = bf16[256,128]{1,0:T(8,128)(2,1)S(1)} collective-permute-done((bf16[256,128]{1,0:T(8,128)(2,1)S(1)}, bf16[256,128]{1,0:T(8,128)(2,1)S(1)}, u32[]{:S(2)}, u32[]{:S(2)}) %collective-permute-start.1) | collective-permute-done | bytes 65568 | tf_op jit(solution)/shard_map/ppermute | solution.py:228
  30.5 1.5 %shard_map.72 = (bf16[2,256,128]{2,1,0:T(8,128)(2,1)}, bf16[8,2,2,144,128]{4,3,2,1,0:T(8,128)(2,1)S(1)}) custom-call(bf16[2,3,256,128]{3,2,1,0:T(8,128)(2,1)S(1)} %get-tuple-element.21.x_ref, bf16[2,3,256,128]{3,2,1,0:T(8,128)(2,1)S(1)} %get-tuple-element.22.h_ref, bf16[2,2,9,128,128]{4,3,2,1,0:T(8,128)(2,1)S(1)} %get-tuple-element.23.w_ref, ...), custom_call_target="tpu_custom_call" | custom-call | flops 603979776 | bytes 1000000 | tf_op jit(solution)/shard_map/pallas_call | solution.py:200
  32.0 17.8 %all_to_all.10 = bf16[8,2,2,144,128]{4,3,2,1,0:T(8,128)(2,1)S(1)} all-to-all(bf16[8,2,2,144,128]{4,3,2,1,0:T(8,128)(2,1)S(1)} %get-tuple-element.38), channel_id=1, replica_groups={{0,1,4,5,8,9,12,13},{2,3,6,7,10,11,14,15},{16,17,20,21,24,25,28,29},{18..., dimensions={0} | all-to-all | bytes 2359296 | tf_op jit(solution)/shard_map/all_to_all | solution.py:339
  49.8 0.2 add_convert_fusion
  49.9 28.8 %all_to_all.11 = bf16[4,144,128]{2,1,0:T(8,128)(2,1)S(1)} all-to-all(bf16[4,144,128]{2,1,0:T(8,128)(2,1)S(1)} %bitcast.10), channel_id=1, replica_groups={{0,2,496,498},{1,3,497,499},{4,6,500,502},{5,7,501,503},{8,10,504,506},..., dimensions={0} | all-to-all | bytes 294912 | tf_op jit(solution)/shard_map/all_to_all | solution.py:341
  78.7 0.7 add_multiply_fusion
Async XLA Ops:
  3.5 11.6 %collective-permute-start.2 = (bf16[256,128]{1,0:T(8,128)(2,1)S(1)}, bf16[256,128]{1,0:T(8,128)(2,1)S(1)}, u32[]{:S(2)}, u32[]{:S(2)}) collective-permute-start(bf16[256,128]{1,0:T(8,128)(2,1)S(1)} %get-tuple-element.27), channel_id=1, source_target_pairs={{16,32},{32,16},{48,64},{64,48},{80,96},{96,80},{112,128},{128,112... | collective-permute-start | bytes 196616 | tf_op jit(solution)/shard_map/ppermute | solution.py:228
  12.8 5.2 %collective-permute-start = (bf16[256,128]{1,0:T(8,128)(2,1)S(1)}, bf16[256,128]{1,0:T(8,128)(2,1)S(1)}, u32[]{:S(2)}, u32[]{:S(2)}) collective-permute-start(bf16[256,128]{1,0:T(8,128)(2,1)S(1)} %get-tuple-element.24), channel_id=1, source_target_pairs={{0,16},{16,0},{32,48},{48,32},{64,80},{80,64},{96,112},{112,96},{1... | collective-permute-start | bytes 196616 | tf_op jit(solution)/shard_map/ppermute | solution.py:228
  15.9 12.1 %collective-permute-start.3 = (bf16[256,128]{1,0:T(8,128)(2,1)S(1)}, bf16[256,128]{1,0:T(8,128)(2,1)S(1)}, u32[]{:S(2)}, u32[]{:S(2)}) collective-permute-start(bf16[256,128]{1,0:T(8,128)(2,1)S(1)} %get-tuple-element.28), channel_id=1, source_target_pairs={{0,16},{16,0},{32,48},{48,32},{64,80},{80,64},{96,112},{112,96},{1... | collective-permute-start | bytes 196616 | tf_op jit(solution)/shard_map/ppermute | solution.py:228
  18.8 11.7 %collective-permute-start.1 = (bf16[256,128]{1,0:T(8,128)(2,1)S(1)}, bf16[256,128]{1,0:T(8,128)(2,1)S(1)}, u32[]{:S(2)}, u32[]{:S(2)}) collective-permute-start(bf16[256,128]{1,0:T(8,128)(2,1)S(1)} %get-tuple-element.25), channel_id=1, source_target_pairs={{16,32},{32,16},{48,64},{64,48},{80,96},{96,80},{112,128},{128,112... | collective-permute-start | bytes 196616 | tf_op jit(solution)/shard_map/ppermute | solution.py:228

commit v5 on v4

v5 whole, which is shorter than its diff:
```python
import functools

import jax
import jax.numpy as jnp
from jax import lax
from jax.experimental import pallas as pl
from jax.experimental.pallas import tpu as pltpu
from jax.sharding import PartitionSpec as P


TAPS = 9
PIECE = 16
PARAMS = pltpu.CompilerParams(vmem_limit_bytes=16 << 20)
BF16, F32 = jnp.bfloat16, jnp.float32


def moved_along_x(value, extent):
    cells, channels = value.shape
    wide = value.astype(F32)
    column = lax.broadcasted_iota(jnp.int32, (cells, channels), 0) & (extent - 1)
    left = jnp.where(column == extent - 1, 0.0, pltpu.roll(wide, cells - 1, 0))
    right = jnp.where(column == 0, 0.0, pltpu.roll(wide, 1, 0))
    return jnp.concatenate([left.astype(value.dtype), value, right.astype(value.dtype)], axis=1)


def down(value, extent):
    return jnp.concatenate([jnp.zeros_like(value[:extent]), value[:-extent]], axis=0)


def up(value, extent):
    return jnp.concatenate([value[extent:], jnp.zeros_like(value[:extent])], axis=0)


def conv_back(moved, w_ref, extent):
    rows = [jnp.concatenate([w_ref[3 * r + c] for c in range(3)], axis=1) for r in range(3)]
    result = lax.dot_general(
        moved,
        jnp.concatenate(rows, axis=0),
        (((1,), (1,)), ((), ())),
        preferred_element_type=F32,
    )
    above, level, below = jnp.split(result, 3, axis=1)
    return level + down(below, extent) + up(above, extent)


def step(g, x_ref, h_ref, w_ref, mg_ref, mh_ref, extent, between=None):
    mg_ref[...] = moved_along_x(g, extent)
    grad_z = conv_back(mg_ref[...], w_ref.at[1], extent)
    grad_h = jnp.where(h_ref[...].astype(F32) > 0, grad_z, 0.0).astype(BF16)
    mh_ref[...] = moved_along_x(grad_h, extent)
    if between is not None:
        between()
    grad_u = conv_back(mh_ref[...], w_ref.at[0], extent)
    passed = jnp.where(x_ref[...].astype(F32) > 0, grad_u, 0.0)
    return (g.astype(F32) + passed).astype(BF16)


def kernel_sums(act_refs, moved_refs, extent):
    rows = []
    for act_ref in act_refs:
        act = jnp.maximum(act_ref[...].astype(F32), 0.0).astype(BF16)
        rows.append(jnp.concatenate([down(act, extent), act, up(act, extent)], axis=1))
    return lax.dot_general(
        jnp.concatenate(rows, axis=0),
        jnp.concatenate([moved[...] for moved in moved_refs], axis=0),
        (((0,), (0,)), ((), ())),
        preferred_element_type=F32,
    )


def pieces(total, pair):
    channels = total.shape[0] // 3
    for k in range(TAPS):
        for start in range(0, channels, PIECE):
            top, left = k // 3 * channels + start, k % 3 * channels
            values = total[top : top + PIECE, left : left + channels]
            yield (pair * TAPS + k) * channels + start, values


def first_kernel(extent, ticks, x_hbm, h_hbm, w_hbm, g_hbm, l_hbm, *refs):
    xs, hs, ws, loss, mg0, mg1, mh0, mh1, gx0, gx1, gs, sems = refs
    position = lax.axis_index("section")
    parity = position & 1
    at_end = (position == 0) | (position == lax.axis_size("section") - 1)
    copies = []

    def fetch(source, target):
        copy = pltpu.make_async_copy(source, target, sems.at[len(copies)])
        copy.start()
        copies.append(copy)

    for slot in (0, 1):
        replica = parity if slot == 0 else 1 - parity
        fetch(g_hbm.at[replica], gs.at[slot])
        fetch(w_hbm.at[replica, 1], ws.at[slot, 1])
        fetch(h_hbm.at[replica * ticks], hs.at[slot, 0])
        fetch(w_hbm.at[replica, 0], ws.at[slot, 0])
        fetch(x_hbm.at[replica * ticks], xs.at[slot, 0])
    for slot in (0, 1):
        replica = parity if slot == 0 else 1 - parity
        later = pl.ds(replica * ticks + 1, ticks - 1)
        fetch(h_hbm.at[later], hs.at[slot, pl.ds(1, ticks - 1)])
        fetch(x_hbm.at[later], xs.at[slot, pl.ds(1, ticks - 1)])
    fetch(l_hbm.at[pl.ds((1 - parity) * (ticks - 1), ticks - 1)], loss)
    for slot, mg_ref, mh_ref, gx_ref in ((0, mg0, mh0, gx0), (1, mg1, mh1, gx1)):
        needed = copies[5 * slot : 5 * slot + 5]

        def wait(some):
            for copy in some:
                copy.wait()

        wait(needed[:3])
        gx_ref[...] = step(
            gs[slot],
            xs.at[slot, 0],
            hs.at[slot, 0],
            ws.at[slot],
            mg_ref,
            mh_ref,
            extent,
            functools.partial(wait, needed[3:]),
        )
    for copy in copies[10:]:
        copy.wait()

    @pl.when(jnp.logical_not(at_end))
    def _():
        loss[...] = jnp.zeros_like(loss)


def middle_kernel(extent, slot, tick, x_ref, h_ref, w_ref, g_ref, *refs):
    g = g_ref[...]
    if slot == 1:
        g = (g.astype(F32) + refs[0][tick - 1].astype(F32)).astype(BF16)
    mg_ref, mh_ref, gx_ref = refs[-3:]
    gx_ref[...] = step(
        g, x_ref.at[slot, tick], h_ref.at[slot, tick], w_ref.at[slot], mg_ref, mh_ref, extent
    )


def even_last_kernel(extent, ticks, x_ref, h_ref, w_ref, g_ref, *refs):
    early = ticks - 1
    moved_h, moved_g = refs[:early], refs[early : 2 * early]
    gx_ref, out_ref, mg_ref, mh_ref = refs[2 * early :]
    gx_ref[...] = step(
        g_ref[...],
        x_ref.at[0, early],
        h_ref.at[0, early],
        w_ref.at[0],
        mg_ref,
        mh_ref,
        extent,
    )
    for pair, act_ref, moved in ((0, x_ref, (*moved_h, mh_ref)), (1, h_ref, (*moved_g, mg_ref))):
        total = kernel_sums([act_ref.at[0, n] for n in range(ticks)], moved, extent)
        for row, value in pieces(total, pair):
            out_ref[row : row + PIECE, :] = value.astype(BF16)


def last_kernel(extent, ticks, parts, x_ref, h_ref, w_ref, g_ref, loss_ref, gx0_ref, sums0_ref, *refs):
    early = ticks - 1
    moved_h, moved_g = refs[:early], refs[early : 2 * early]
    edge_hbm, out_ref, mg_ref, mh_ref, gx1_ref, sems = refs[2 * early :]
    position = lax.axis_index("section")
    parity = position & 1
    g = (g_ref[...].astype(F32) + loss_ref[early - 1].astype(F32)).astype(BF16)
    copies = [
        pltpu.make_async_copy(gx0_ref, edge_hbm.at[parity], sems.at[0]),
        pltpu.make_async_copy(gx1_ref, edge_hbm.at[1 - parity], sems.at[1]),
    ]
    copies[0].start()
    gx1_ref[...] = step(
        g, x_ref.at[1, early], h_ref.at[1, early], w_ref.at[1], mg_ref, mh_ref, extent
    )
    members, _, later, rows_each, _ = out_ref.shape
    upper = (position >= lax.axis_size("section") // 2).astype(jnp.int32)
    half0, half1 = (parity + upper) & 1, (1 - parity + upper) & 1

    def put(row, half, value):
        shard, inner = row // rows_each, row % rows_each
        block, pair_at = shard // (2 * later), shard % (2 * later)
        member = block * (members // parts) + pair_at % 2
        out_ref[member, half, pair_at // 2, inner : inner + value.shape[0], :] = value

    for row in range(0, sums0_ref.shape[0], rows_each):
        put(row, half0, sums0_ref[row : row + rows_each, :])
    copies[1].start()
    for pair, act_ref, moved in ((0, x_ref, (*moved_h, mh_ref)), (1, h_ref, (*moved_g, mg_ref))):
        total = kernel_sums([act_ref.at[1, n] for n in range(ticks)], moved, extent)
        for row, value in pieces(total, pair):
            put(row, half1, value.astype(BF16))
    for copy in copies:
        copy.wait()


def call(body, steps, in_specs, out_shape, scratch, args, hbm_outs=0):
    cells, channels = args[0].shape[-2:]
    return pl.pallas_call(
        body,
        in_specs=in_specs,
        out_specs=[in_hbm()] * hbm_outs + [vmem()] * (len(out_shape) - hbm_outs),
        out_shape=out_shape,
        scratch_shapes=scratch,
        compiler_params=PARAMS,
        cost_estimate=pl.CostEstimate(
            flops=4 * steps * cells * TAPS * channels * channels,
            bytes_accessed=1000000,
            transcendentals=0,
        ),
    )(*args)


def vmem():
    return pl.BlockSpec(memory_space=pltpu.VMEM)


def in_hbm():
    return pl.BlockSpec(memory_space=pltpu.HBM)


def exchange(value, offset):
    total = lax.axis_size("section")
    pairs = []
    for low in range(offset, total - 1, 2):
        pairs += [(low, low + 1), (low + 1, low)]
    return lax.ppermute(value, "section", pairs)


def on_device(factors, saved_x, saved_h, kernels, grad_in, loss_grads):
    return whole(factors, saved_x, saved_h, kernels, grad_in, loss_grads)


def whole(factors, saved_x, saved_h, kernels, grad_in, loss_grads):
    ticks = saved_x.shape[1]
    extent, channels = saved_x.shape[4], saved_x.shape[6]
    cells = extent * extent
    sections = lax.axis_size("section")
    outer, inner = factors
    later, shards = inner // 2, outer * inner
    rows = 2 * TAPS * channels
    field = (cells, channels)

    def shape(*lead, tail=field):
        return jax.ShapeDtypeStruct((*lead, *tail), BF16)

    moved = shape(tail=(cells, 3 * channels))
    scratch = [pltpu.VMEM(moved.shape, BF16)] * 2

    xs, hs, ws, loss, mg0, mg1, mh0, mh1, out0, out1 = call(
        functools.partial(first_kernel, extent, ticks),
        2,
        [in_hbm()] * 5,
        [
            shape(2, ticks),
            shape(2, ticks),
            shape(*kernels.shape[1:-2], tail=(channels, channels)),
            shape(ticks - 1),
            *[moved] * 4,
            *[shape()] * 2,
        ],
        [pltpu.VMEM((2, *field), BF16), pltpu.SemaphoreType.DMA((15,))],
        [
            pltpu.with_memory_space_constraint(value, pltpu.HBM)
            for value in (
                saved_x.reshape(-1, *field),
                saved_h.reshape(-1, *field),
                kernels[0],
                grad_in.reshape(-1, *field),
                loss_grads.reshape(-1, *field),
            )
        ],
    )
    mg, mh = [[mg0], [mg1]], [[mh0], [mh1]]
    for tick in range(1, ticks):
        far = exchange(out0, 1)
        near = exchange(out1, 0)
        if tick == ticks - 1:
            break
        mg0, mh0, out0 = call(
            functools.partial(middle_kernel, extent, 0, tick),
            1,
            [vmem()] * 4,
            [moved, moved, shape()],
            [],
            (xs, hs, ws, near),
        )
        mg1, mh1, out1 = call(
            functools.partial(middle_kernel, extent, 1, tick),
            1,
            [vmem()] * 5,
            [moved, moved, shape()],
            [],
            (xs, hs, ws, far, loss),
        )
        for slot, used, made in ((0, mg0, mh0), (1, mg1, mh1)):
            mg[slot].append(used)
            mh[slot].append(made)
    out0, sums0 = call(
        functools.partial(even_last_kernel, extent, ticks),
        1 + ticks,
        [vmem()] * (4 + 2 * (ticks - 1)),
        [shape(), shape(tail=(rows, channels))],
        scratch,
        (xs, hs, ws, near, *mh[0], *mg[0]),
    )
    edge, both = call(
        functools.partial(last_kernel, extent, ticks, outer),
        1 + ticks,
        [vmem()] * (7 + 2 * (ticks - 1)),
        [shape(2), shape(2 * outer, 2, later, rows // shards, tail=(channels,))],
        [*scratch, pltpu.VMEM(field, BF16), pltpu.SemaphoreType.DMA((2,))],
        (xs, hs, ws, far, loss, out0, sums0, *mh[1], *mg[1]),
        hbm_outs=1,
    )
    edge_grads = edge.reshape(2, 1, 1, extent, extent, channels)

    def shard(block, far, near):
        return (block * later + far) * 2 + near

    first_groups = [
        [shard(block, far, near) for block in range(outer) for near in range(2)]
        for far in range(later)
    ]
    second_groups = [
        [
            section * shards + shard(block, far, near)
            for section in (low, sections - 1 - low)
            for far in range(later)
        ]
        for low in range(sections // 2)
        for block in range(outer)
        for near in range(2)
    ]

    def total(value):
        parts = [value[n].astype(F32) for n in range(value.shape[0])]
        return functools.reduce(lambda a, b: a + b, parts)

    both = lax.all_to_all(both, "dp", 0, 0, axis_index_groups=first_groups, tiled=True)
    both = total(both).astype(BF16).reshape(2 * later, rows // shards, channels)
    both = lax.all_to_all(
        both, ("section", "dp"), 0, 0, axis_index_groups=second_groups, tiled=True
    )
    kernel_grads = (total(both) * (1.0 / float(cells)))[None]
    return (kernel_grads, edge_grads)


def solution(mesh):
    shards = mesh.shape["dp"]
    outer = next(f for f in (4, 2, 1) if shards % f == 0)
    return jax.shard_map(
        functools.partial(on_device, (outer, shards // outer)),
        mesh=mesh,
        in_specs=(
            P(None, None, "section", "dp", None, None, None),
            P(None, None, "section", "dp", None, None, None),
            P("section", None, None, None, None, None),
            P(None, "section", "dp", None, None, None),
            P(None, None, "dp", None, None, None),
        ),
        out_specs=(P("section", "dp", None), P(None, "section", "dp", None, None, None)),
        check_vma=False,
    )
```

time: 79.7 us -> 78.7 us (0.987)
  Pallas kernels: 7.27 us -> 6.14 us
    pallas_call x5, Pallas kernels: 7.27 us -> 6.14 us  [call(): pl.pallas_call(body, in_specs=in_specs, out_specs=[in_hbm()] * hbm_outs +...]
  transfers between devices with their start and end apart: 4 -> 4, of which waited for: 2 -> 2; matrix products, arithmetic and copies ran while one was open for 0% -> 0% of each run, Pallas kernels for 4% -> 3%
where the time goes in v5:
time: 78.7 us; the launch traced here: 78.4 us
  blocking collectives  46.6 us (59%)
  starting transfers between devices  22.5 us (29%)
  Pallas kernels  6.14 us (8%)
  waiting for transfers between devices  1.69 us (2%)
  other arithmetic  0.81 us (1%)
    all_to_all x1, blocking collectives, whole(): lax.all_to_all(both, ('section', 'dp'), 0, 0, axis_index_groups=second_gr...  28.8 us
    ppermute x4, starting transfers between devices, exchange(): return lax.ppermute(value, 'section', pairs)  22.5 us
    all_to_all x1, blocking collectives, whole(): lax.all_to_all(both, 'dp', 0, 0, axis_index_groups=first_groups, tiled=True)  17.8 us
    pallas_call x5, Pallas kernels, call(): pl.pallas_call(body, in_specs=in_specs, out_specs=[in_hbm()] * hbm_outs +...  6.14 us
    ppermute x4, waiting for transfers between devices, exchange(): return lax.ppermute(value, 'section', pairs)  1.69 us
  transfers between devices with their start and end apart: 4, of which 2 were waited for; matrix products, arithmetic and copies ran while one was open for 0% of the time, Pallas kernels for 3%

profile of v5, /device:TPU:7, one launch (start us, length us, event | category | flops | bytes accessed | tf_op | source)
XLA Modules:
  0.0 78.4 jit_solution(11163999714961681539)
XLA Ops:
  0.6 2.5 %shard_map.68 = (bf16[2,3,256,128]{3,2,1,0:T(8,128)(2,1)S(1)}, bf16[2,3,256,128]{3,2,1,0:T(8,128)(2,1)S(1)}, bf16[2,2,9,128,128]{4,3,2,1,0:T(8,128)(2,1)S(1)}, b...) custom-call(bf16[6,256,128]{2,1,0:T(8,128)(2,1)} %bitcast.11, ...), custom_call_target="tpu_custom_call" | custom-call | flops 301989888 | bytes 1000000 | tf_op jit(solution)/shard_map/pallas_call | solution.py:198
  3.1 9.3 %collective-permute-start.2 = (bf16[256,128]{1,0:T(8,128)(2,1)S(1)}, bf16[256,128]{1,0:T(8,128)(2,1)S(1)}, u32[]{:S(2)}, u32[]{:S(2)}) collective-permute-start(bf16[256,128]{1,0:T(8,128)(2,1)S(1)} %get-tuple-element.28), channel_id=1, source_target_pairs={{16,32},{32,16},{48,64},{64,48},{80,96},{96,80},{112,128},{128,112... | collective-permute-start | bytes 196616 | tf_op jit(solution)/shard_map/ppermute | solution.py:226
  12.4 1.9 %collective-permute-start = (bf16[256,128]{1,0:T(8,128)(2,1)S(1)}, bf16[256,128]{1,0:T(8,128)(2,1)S(1)}, u32[]{:S(2)}, u32[]{:S(2)}) collective-permute-start(bf16[256,128]{1,0:T(8,128)(2,1)S(1)} %get-tuple-element.25), channel_id=1, source_target_pairs={{0,16},{16,0},{32,48},{48,32},{64,80},{80,64},{96,112},{112,96},{1... | collective-permute-start | bytes 196616 | tf_op jit(solution)/shard_map/ppermute | solution.py:226
  14.4 0.4 collective-permute-done.2.g_ref
  14.7 0.6 shard_map.70
  15.3 2.0 %collective-permute-start.3 = (bf16[256,128]{1,0:T(8,128)(2,1)S(1)}, bf16[256,128]{1,0:T(8,128)(2,1)S(1)}, u32[]{:S(2)}, u32[]{:S(2)}) collective-permute-start(bf16[256,128]{1,0:T(8,128)(2,1)S(1)} %get-tuple-element.29), channel_id=1, source_target_pairs={{0,16},{16,0},{32,48},{48,32},{64,80},{80,64},{96,112},{112,96},{1... | collective-permute-start | bytes 196616 | tf_op jit(solution)/shard_map/ppermute | solution.py:226
  17.4 0.0 collective-permute-done.g_ref
  17.4 0.6 shard_map.69
  17.9 9.2 %collective-permute-start.1 = (bf16[256,128]{1,0:T(8,128)(2,1)S(1)}, bf16[256,128]{1,0:T(8,128)(2,1)S(1)}, u32[]{:S(2)}, u32[]{:S(2)}) collective-permute-start(bf16[256,128]{1,0:T(8,128)(2,1)S(1)} %get-tuple-element.26), channel_id=1, source_target_pairs={{16,32},{32,16},{48,64},{64,48},{80,96},{96,80},{112,128},{128,112... | collective-permute-start | bytes 196616 | tf_op jit(solution)/shard_map/ppermute | solution.py:226
  27.1 0.0 collective-permute-done.3.g_ref
  27.1 1.2 %shard_map.71 = (bf16[256,128]{1,0:T(8,128)(2,1)S(1)}, bf16[2304,128]{1,0:T(8,128)(2,1)S(1)}) custom-call(bf16[2,3,256,128]{3,2,1,0:T(8,128)(2,1)S(1)} %get-tuple-element.22.x_ref, bf16[2,3,256,128]{3,2,1,0:T(8,128)(2,1)S(1)} %get-tuple-element.23.h_ref, bf16[2,2,9,128,128]{4,3,2,1,0:T(8,128)(2,1)S(1)} %get-tuple-element.24.w_ref, ...), custom_call_target="tpu_custom_call" | custom-call | flops 603979776 | bytes 1000000 | tf_op jit(solution)/shard_map/pallas_call | solution.py:198
  28.3 1.3 %collective-permute-done.1.g_ref = bf16[256,128]{1,0:T(8,128)(2,1)S(1)} collective-permute-done((bf16[256,128]{1,0:T(8,128)(2,1)S(1)}, bf16[256,128]{1,0:T(8,128)(2,1)S(1)}, u32[]{:S(2)}, u32[]{:S(2)}) %collective-permute-start.1) | collective-permute-done | bytes 65568 | tf_op jit(solution)/shard_map/ppermute | solution.py:226
  29.6 1.3 %shard_map.72 = (bf16[2,256,128]{2,1,0:T(8,128)(2,1)}, bf16[8,2,2,144,128]{4,3,2,1,0:T(8,128)(2,1)S(1)}) custom-call(bf16[2,3,256,128]{3,2,1,0:T(8,128)(2,1)S(1)} %get-tuple-element.22.x_ref, bf16[2,3,256,128]{3,2,1,0:T(8,128)(2,1)S(1)} %get-tuple-element.23.h_ref, bf16[2,2,9,128,128]{4,3,2,1,0:T(8,128)(2,1)S(1)} %get-tuple-element.24.w_ref, ...), custom_call_target="tpu_custom_call" | custom-call | flops 603979776 | bytes 1000000 | tf_op jit(solution)/shard_map/pallas_call | solution.py:198
  31.0 17.8 %all_to_all.10 = bf16[8,2,2,144,128]{4,3,2,1,0:T(8,128)(2,1)S(1)} all-to-all(bf16[8,2,2,144,128]{4,3,2,1,0:T(8,128)(2,1)S(1)} %get-tuple-element.40), channel_id=1, replica_groups={{0,1,4,5,8,9,12,13},{2,3,6,7,10,11,14,15},{16,17,20,21,24,25,28,29},{18..., dimensions={0} | all-to-all | bytes 2359296 | tf_op jit(solution)/shard_map/all_to_all | solution.py:339
  48.8 0.2 add_convert_fusion
  49.0 28.8 %all_to_all.11 = bf16[4,144,128]{2,1,0:T(8,128)(2,1)S(1)} all-to-all(bf16[4,144,128]{2,1,0:T(8,128)(2,1)S(1)} %bitcast.10), channel_id=1, replica_groups={{0,2,496,498},{1,3,497,499},{4,6,500,502},{5,7,501,503},{8,10,504,506},..., dimensions={0} | all-to-all | bytes 294912 | tf_op jit(solution)/shard_map/all_to_all | solution.py:341
  77.8 0.7 add_multiply_fusion
Async XLA Ops:
  3.1 11.6 %collective-permute-start.2 = (bf16[256,128]{1,0:T(8,128)(2,1)S(1)}, bf16[256,128]{1,0:T(8,128)(2,1)S(1)}, u32[]{:S(2)}, u32[]{:S(2)}) collective-permute-start(bf16[256,128]{1,0:T(8,128)(2,1)S(1)} %get-tuple-element.28), channel_id=1, source_target_pairs={{16,32},{32,16},{48,64},{64,48},{80,96},{96,80},{112,128},{128,112... | collective-permute-start | bytes 196616 | tf_op jit(solution)/shard_map/ppermute | solution.py:226
  12.4 4.9 %collective-permute-start = (bf16[256,128]{1,0:T(8,128)(2,1)S(1)}, bf16[256,128]{1,0:T(8,128)(2,1)S(1)}, u32[]{:S(2)}, u32[]{:S(2)}) collective-permute-start(bf16[256,128]{1,0:T(8,128)(2,1)S(1)} %get-tuple-element.25), channel_id=1, source_target_pairs={{0,16},{16,0},{32,48},{48,32},{64,80},{80,64},{96,112},{112,96},{1... | collective-permute-start | bytes 196616 | tf_op jit(solution)/shard_map/ppermute | solution.py:226
  15.3 11.8 %collective-permute-start.3 = (bf16[256,128]{1,0:T(8,128)(2,1)S(1)}, bf16[256,128]{1,0:T(8,128)(2,1)S(1)}, u32[]{:S(2)}, u32[]{:S(2)}) collective-permute-start(bf16[256,128]{1,0:T(8,128)(2,1)S(1)} %get-tuple-element.29), channel_id=1, source_target_pairs={{0,16},{16,0},{32,48},{48,32},{64,80},{80,64},{96,112},{112,96},{1... | collective-permute-start | bytes 196616 | tf_op jit(solution)/shard_map/ppermute | solution.py:226
  17.9 11.7 %collective-permute-start.1 = (bf16[256,128]{1,0:T(8,128)(2,1)S(1)}, bf16[256,128]{1,0:T(8,128)(2,1)S(1)}, u32[]{:S(2)}, u32[]{:S(2)}) collective-permute-start(bf16[256,128]{1,0:T(8,128)(2,1)S(1)} %get-tuple-element.26), channel_id=1, source_target_pairs={{16,32},{32,16},{48,64},{64,48},{80,96},{96,80},{112,128},{128,112... | collective-permute-start | bytes 196616 | tf_op jit(solution)/shard_map/ppermute | solution.py:226

commit v6 on v5

--- a/solution.py
+++ b/solution.py
@@ -89,39 +89,42 @@
         copy.start()
         copies.append(copy)
 
-    for slot in (0, 1):
+    def fetch_first(slot):
         replica = parity if slot == 0 else 1 - parity
         fetch(g_hbm.at[replica], gs.at[slot])
         fetch(w_hbm.at[replica, 1], ws.at[slot, 1])
         fetch(h_hbm.at[replica * ticks], hs.at[slot, 0])
         fetch(w_hbm.at[replica, 0], ws.at[slot, 0])
         fetch(x_hbm.at[replica * ticks], xs.at[slot, 0])
-    for slot in (0, 1):
-        replica = parity if slot == 0 else 1 - parity
-        later = pl.ds(replica * ticks + 1, ticks - 1)
-        fetch(h_hbm.at[later], hs.at[slot, pl.ds(1, ticks - 1)])
-        fetch(x_hbm.at[later], xs.at[slot, pl.ds(1, ticks - 1)])
-    fetch(l_hbm.at[pl.ds((1 - parity) * (ticks - 1), ticks - 1)], loss)
-    for slot, mg_ref, mh_ref, gx_ref in ((0, mg0, mh0, gx0), (1, mg1, mh1, gx1)):
-        needed = copies[5 * slot : 5 * slot + 5]
-
-        def wait(some):
-            for copy in some:
-                copy.wait()
-
-        wait(needed[:3])
-        gx_ref[...] = step(
-            gs[slot],
-            xs.at[slot, 0],
-            hs.at[slot, 0],
-            ws.at[slot],
-            mg_ref,
-            mh_ref,
-            extent,
-            functools.partial(wait, needed[3:]),
-        )
-    for copy in copies[10:]:
-        copy.wait()
+
+    def fetch_later():
+        for slot in (0, 1):
+            replica = parity if slot == 0 else 1 - parity
+            later = pl.ds(replica * ticks + 1, ticks - 1)
+            fetch(h_hbm.at[later], hs.at[slot, pl.ds(1, ticks - 1)])
+            fetch(x_hbm.at[later], xs.at[slot, pl.ds(1, ticks - 1)])
+        fetch(l_hbm.at[pl.ds((1 - parity) * (ticks - 1), ticks - 1)], loss)
+
+    def wait(first, last):
+        for copy in copies[first:last]:
+            copy.wait()
+
+    fetch_first(0)
+    wait(0, 3)
+    fetch_first(1)
+
+    def middle_of_slot_0():
+        wait(3, 5)
+        fetch_later()
+
+    gx0[...] = step(
+        gs[0], xs.at[0, 0], hs.at[0, 0], ws.at[0], mg0, mh0, extent, middle_of_slot_0
+    )
+    wait(5, 8)
+    gx1[...] = step(
+        gs[1], xs.at[1, 0], hs.at[1, 0], ws.at[1], mg1, mh1, extent, lambda: wait(8, 10)
+    )
+    wait(10, len(copies))
 
     @pl.when(jnp.logical_not(at_end))
     def _():
@@ -138,10 +141,18 @@
     )
 
 
-def even_last_kernel(extent, ticks, x_ref, h_ref, w_ref, g_ref, *refs):
-    early = ticks - 1
-    moved_h, moved_g = refs[:early], refs[early : 2 * early]
-    gx_ref, out_ref, mg_ref, mh_ref = refs[2 * early :]
+def early_kernel(extent, early, x_ref, h_ref, *refs):
+    out_refs = refs[-2:]
+    for slot in (0, 1):
+        mine = refs[2 * early * slot : 2 * early * (slot + 1)]
+        for pair, act_ref, moved in ((0, x_ref, mine[:early]), (1, h_ref, mine[early:])):
+            total = kernel_sums([act_ref.at[slot, n] for n in range(early)], moved, extent)
+            for row, value in pieces(total, pair):
+                out_refs[slot][row : row + PIECE, :] = value
+
+
+def even_last_kernel(extent, early, x_ref, h_ref, w_ref, g_ref, acc_ref, *refs):
+    gx_ref, out_ref, mg_ref, mh_ref = refs
     gx_ref[...] = step(
         g_ref[...],
         x_ref.at[0, early],
@@ -151,16 +162,15 @@
         mh_ref,
         extent,
     )
-    for pair, act_ref, moved in ((0, x_ref, (*moved_h, mh_ref)), (1, h_ref, (*moved_g, mg_ref))):
-        total = kernel_sums([act_ref.at[0, n] for n in range(ticks)], moved, extent)
+    for pair, act_ref, moved_ref in ((0, x_ref, mh_ref), (1, h_ref, mg_ref)):
+        total = kernel_sums([act_ref.at[0, early]], [moved_ref], extent)
         for row, value in pieces(total, pair):
+            value = value + acc_ref[row : row + PIECE, :]
             out_ref[row : row + PIECE, :] = value.astype(BF16)
 
 
-def last_kernel(extent, ticks, parts, x_ref, h_ref, w_ref, g_ref, loss_ref, gx0_ref, sums0_ref, *refs):
-    early = ticks - 1
-    moved_h, moved_g = refs[:early], refs[early : 2 * early]
-    edge_hbm, out_ref, mg_ref, mh_ref, gx1_ref, sems = refs[2 * early :]
+def last_kernel(extent, early, parts, x_ref, h_ref, w_ref, g_ref, loss_ref, *refs):
+    gx0_ref, sums0_ref, acc_ref, edge_hbm, out_ref, mg_ref, mh_ref, gx1_ref, sems = refs
     position = lax.axis_index("section")
     parity = position & 1
     g = (g_ref[...].astype(F32) + loss_ref[early - 1].astype(F32)).astype(BF16)
@@ -185,10 +195,10 @@
     for row in range(0, sums0_ref.shape[0], rows_each):
         put(row, half0, sums0_ref[row : row + rows_each, :])
     copies[1].start()
-    for pair, act_ref, moved in ((0, x_ref, (*moved_h, mh_ref)), (1, h_ref, (*moved_g, mg_ref))):
-        total = kernel_sums([act_ref.at[1, n] for n in range(ticks)], moved, extent)
+    for pair, act_ref, moved_ref in ((0, x_ref, mh_ref), (1, h_ref, mg_ref)):
+        total = kernel_sums([act_ref.at[1, early]], [moved_ref], extent)
         for row, value in pieces(total, pair):
-            put(row, half1, value.astype(BF16))
+            put(row, half1, (value + acc_ref[row : row + PIECE, :]).astype(BF16))
     for copy in copies:
         copy.wait()
 
@@ -295,21 +305,31 @@
         for slot, used, made in ((0, mg0, mh0), (1, mg1, mh1)):
             mg[slot].append(used)
             mh[slot].append(made)
+    early = ticks - 1
+    sums = jax.ShapeDtypeStruct((rows, channels), F32)
+    acc0, acc1 = call(
+        functools.partial(early_kernel, extent, early),
+        2 * early,
+        [vmem()] * (2 + 4 * early),
+        [sums, sums],
+        [],
+        (xs, hs, *mh[0], *mg[0], *mh[1], *mg[1]),
+    )
     out0, sums0 = call(
-        functools.partial(even_last_kernel, extent, ticks),
-        1 + ticks,
-        [vmem()] * (4 + 2 * (ticks - 1)),
+        functools.partial(even_last_kernel, extent, early),
+        2,
+        [vmem()] * 5,
         [shape(), shape(tail=(rows, channels))],
         scratch,
-        (xs, hs, ws, near, *mh[0], *mg[0]),
+        (xs, hs, ws, near, acc0),
     )
     edge, both = call(
-        functools.partial(last_kernel, extent, ticks, outer),
-        1 + ticks,
-        [vmem()] * (7 + 2 * (ticks - 1)),
+        functools.partial(last_kernel, extent, early, outer),
+        2,
+        [vmem()] * 8,
         [shape(2), shape(2 * outer, 2, later, rows // shards, tail=(channels,))],
         [*scratch, pltpu.VMEM(field, BF16), pltpu.SemaphoreType.DMA((2,))],
-        (xs, hs, ws, far, loss, out0, sums0, *mh[1], *mg[1]),
+        (xs, hs, ws, far, loss, out0, sums0, acc1),
         hbm_outs=1,
     )
     edge_grads = edge.reshape(2, 1, 1, extent, extent, channels)

time: 78.7 us -> 79 us (level)
  Pallas kernels: 6.14 us -> 6.99 us
    pallas_call x5 -> x6, Pallas kernels: 6.14 us -> 6.99 us  [call(): pl.pallas_call(body, in_specs=in_specs, out_specs=[in_hbm()] * hbm_outs +...]
  transfers between devices with their start and end apart: 4 -> 4, of which waited for: 2 -> 2; matrix products, arithmetic and copies ran while one was open for 0% -> 0% of each run, Pallas kernels for 3% -> 4%
where the time goes in v6:
time: 79 us; the launch traced here: 78.7 us
  blocking collectives  46.7 us (59%)
  starting transfers between devices  22.4 us (28%)
  Pallas kernels  6.99 us (9%)
  waiting for transfers between devices  1.06 us (1%)
  other arithmetic  0.81 us (1%)
    all_to_all x1, blocking collectives, whole(): lax.all_to_all(both, ('section', 'dp'), 0, 0, axis_index_groups=second_gr...  28.9 us
    ppermute x4, starting transfers between devices, exchange(): return lax.ppermute(value, 'section', pairs)  22.4 us
    all_to_all x1, blocking collectives, whole(): lax.all_to_all(both, 'dp', 0, 0, axis_index_groups=first_groups, tiled=True)  17.8 us
    pallas_call x6, Pallas kernels, call(): pl.pallas_call(body, in_specs=in_specs, out_specs=[in_hbm()] * hbm_outs +...  6.99 us
  transfers between devices with their start and end apart: 4, of which 2 were waited for; matrix products, arithmetic and copies ran while one was open for 0% of the time, Pallas kernels for 4%

profile of v6, /device:TPU:7, one launch (start us, length us, event | category | flops | bytes accessed | tf_op | source)
XLA Modules:
  0.0 78.7 jit_solution(11303325581185169980)
XLA Ops:
  0.6 2.9 %shard_map.68 = (bf16[2,3,256,128]{3,2,1,0:T(8,128)(2,1)S(1)}, bf16[2,3,256,128]{3,2,1,0:T(8,128)(2,1)S(1)}, bf16[2,2,9,128,128]{4,3,2,1,0:T(8,128)(2,1)S(1)}, b...) custom-call(bf16[6,256,128]{2,1,0:T(8,128)(2,1)} %bitcast.11, ...), custom_call_target="tpu_custom_call" | custom-call | flops 301989888 | bytes 1000000 | tf_op jit(solution)/shard_map/pallas_call | solution.py:208
  3.5 9.3 %collective-permute-start.2 = (bf16[256,128]{1,0:T(8,128)(2,1)S(1)}, bf16[256,128]{1,0:T(8,128)(2,1)S(1)}, u32[]{:S(2)}, u32[]{:S(2)}) collective-permute-start(bf16[256,128]{1,0:T(8,128)(2,1)S(1)} %get-tuple-element.30), channel_id=1, source_target_pairs={{16,32},{32,16},{48,64},{64,48},{80,96},{96,80},{112,128},{128,112... | collective-permute-start | bytes 196616 | tf_op jit(solution)/shard_map/ppermute | solution.py:236
  12.8 1.9 %collective-permute-start = (bf16[256,128]{1,0:T(8,128)(2,1)S(1)}, bf16[256,128]{1,0:T(8,128)(2,1)S(1)}, u32[]{:S(2)}, u32[]{:S(2)}) collective-permute-start(bf16[256,128]{1,0:T(8,128)(2,1)S(1)} %get-tuple-element.27), channel_id=1, source_target_pairs={{0,16},{16,0},{32,48},{48,32},{64,80},{80,64},{96,112},{112,96},{1... | collective-permute-start | bytes 196616 | tf_op jit(solution)/shard_map/ppermute | solution.py:236
  14.7 0.4 collective-permute-done.2.g_ref
  15.1 0.6 shard_map.70
  15.7 2.0 %collective-permute-start.3 = (bf16[256,128]{1,0:T(8,128)(2,1)S(1)}, bf16[256,128]{1,0:T(8,128)(2,1)S(1)}, u32[]{:S(2)}, u32[]{:S(2)}) collective-permute-start(bf16[256,128]{1,0:T(8,128)(2,1)S(1)} %get-tuple-element.31), channel_id=1, source_target_pairs={{0,16},{16,0},{32,48},{48,32},{64,80},{80,64},{96,112},{112,96},{1... | collective-permute-start | bytes 196616 | tf_op jit(solution)/shard_map/ppermute | solution.py:236
  17.7 0.0 collective-permute-done.g_ref
  17.7 0.6 shard_map.69
  18.3 9.2 %collective-permute-start.1 = (bf16[256,128]{1,0:T(8,128)(2,1)S(1)}, bf16[256,128]{1,0:T(8,128)(2,1)S(1)}, u32[]{:S(2)}, u32[]{:S(2)}) collective-permute-start(bf16[256,128]{1,0:T(8,128)(2,1)S(1)} %get-tuple-element.28), channel_id=1, source_target_pairs={{16,32},{32,16},{48,64},{64,48},{80,96},{96,80},{112,128},{128,112... | collective-permute-start | bytes 196616 | tf_op jit(solution)/shard_map/ppermute | solution.py:236
  27.5 1.0 %shard_map.71 = (f32[2304,128]{1,0:T(8,128)S(1)}, f32[2304,128]{1,0:T(8,128)S(1)}) custom-call(bf16[2,3,256,128]{3,2,1,0:T(8,128)(2,1)S(1)} %get-tuple-element.24.x_ref, bf16[2,3,256,128]{3,2,1,0:T(8,128)(2,1)S(1)} %get-tuple-element.25.h_ref, bf16[256,384]{1,0:T(8,128)(2,1)S(1)} %get-tuple-element.32.refs_0_, ...), custom_call_target="tpu_custom_call" | custom-call | flops 603979776 | bytes 1000000 | tf_op jit(solution)/shard_map/pallas_call | solution.py:208
  28.5 0.0 collective-permute-done.3.g_ref
  28.5 0.8 shard_map.72
  29.3 0.7 collective-permute-done.1.g_ref
  30.0 1.2 %shard_map.73 = (bf16[2,256,128]{2,1,0:T(8,128)(2,1)}, bf16[8,2,2,144,128]{4,3,2,1,0:T(8,128)(2,1)S(1)}) custom-call(bf16[2,3,256,128]{3,2,1,0:T(8,128)(2,1)S(1)} %get-tuple-element.24.x_ref, bf16[2,3,256,128]{3,2,1,0:T(8,128)(2,1)S(1)} %get-tuple-element.25.h_ref, bf16[2,2,9,128,128]{4,3,2,1,0:T(8,128)(2,1)S(1)} %get-tuple-element.26.w_ref, ...), custom_call_target="tpu_custom_call" | custom-call | flops 301989888 | bytes 1000000 | tf_op jit(solution)/shard_map/pallas_call | solution.py:208
  31.2 17.8 %all_to_all.10 = bf16[8,2,2,144,128]{4,3,2,1,0:T(8,128)(2,1)S(1)} all-to-all(bf16[8,2,2,144,128]{4,3,2,1,0:T(8,128)(2,1)S(1)} %get-tuple-element.44), channel_id=1, replica_groups={{0,1,4,5,8,9,12,13},{2,3,6,7,10,11,14,15},{16,17,20,21,24,25,28,29},{18..., dimensions={0} | all-to-all | bytes 2359296 | tf_op jit(solution)/shard_map/all_to_all | solution.py:359
  49.0 0.2 add_convert_fusion
  49.2 28.9 %all_to_all.11 = bf16[4,144,128]{2,1,0:T(8,128)(2,1)S(1)} all-to-all(bf16[4,144,128]{2,1,0:T(8,128)(2,1)S(1)} %bitcast.10), channel_id=1, replica_groups={{0,2,496,498},{1,3,497,499},{4,6,500,502},{5,7,501,503},{8,10,504,506},..., dimensions={0} | all-to-all | bytes 294912 | tf_op jit(solution)/shard_map/all_to_all | solution.py:361
  78.1 0.7 add_multiply_fusion
Async XLA Ops:
  3.5 11.6 %collective-permute-start.2 = (bf16[256,128]{1,0:T(8,128)(2,1)S(1)}, bf16[256,128]{1,0:T(8,128)(2,1)S(1)}, u32[]{:S(2)}, u32[]{:S(2)}) collective-permute-start(bf16[256,128]{1,0:T(8,128)(2,1)S(1)} %get-tuple-element.30), channel_id=1, source_target_pairs={{16,32},{32,16},{48,64},{64,48},{80,96},{96,80},{112,128},{128,112... | collective-permute-start | bytes 196616 | tf_op jit(solution)/shard_map/ppermute | solution.py:236
  12.8 4.9 %collective-permute-start = (bf16[256,128]{1,0:T(8,128)(2,1)S(1)}, bf16[256,128]{1,0:T(8,128)(2,1)S(1)}, u32[]{:S(2)}, u32[]{:S(2)}) collective-permute-start(bf16[256,128]{1,0:T(8,128)(2,1)S(1)} %get-tuple-element.27), channel_id=1, source_target_pairs={{0,16},{16,0},{32,48},{48,32},{64,80},{80,64},{96,112},{112,96},{1... | collective-permute-start | bytes 196616 | tf_op jit(solution)/shard_map/ppermute | solution.py:236
  15.7 12.9 %collective-permute-start.3 = (bf16[256,128]{1,0:T(8,128)(2,1)S(1)}, bf16[256,128]{1,0:T(8,128)(2,1)S(1)}, u32[]{:S(2)}, u32[]{:S(2)}) collective-permute-start(bf16[256,128]{1,0:T(8,128)(2,1)S(1)} %get-tuple-element.31), channel_id=1, source_target_pairs={{0,16},{16,0},{32,48},{48,32},{64,80},{80,64},{96,112},{112,96},{1... | collective-permute-start | bytes 196616 | tf_op jit(solution)/shard_map/ppermute | solution.py:236
  18.3 11.7 %collective-permute-start.1 = (bf16[256,128]{1,0:T(8,128)(2,1)S(1)}, bf16[256,128]{1,0:T(8,128)(2,1)S(1)}, u32[]{:S(2)}, u32[]{:S(2)}) collective-permute-start(bf16[256,128]{1,0:T(8,128)(2,1)S(1)} %get-tuple-element.28), channel_id=1, source_target_pairs={{16,32},{32,16},{48,64},{64,48},{80,96},{96,80},{112,128},{128,112... | collective-permute-start | bytes 196616 | tf_op jit(solution)/shard_map/ppermute | solution.py:236

commit v7 on v6

--- a/solution.py
+++ b/solution.py
@@ -89,36 +89,27 @@
         copy.start()
         copies.append(copy)
 
-    def fetch_first(slot):
+    for slot in (0, 1):
         replica = parity if slot == 0 else 1 - parity
         fetch(g_hbm.at[replica], gs.at[slot])
         fetch(w_hbm.at[replica, 1], ws.at[slot, 1])
         fetch(h_hbm.at[replica * ticks], hs.at[slot, 0])
         fetch(w_hbm.at[replica, 0], ws.at[slot, 0])
         fetch(x_hbm.at[replica * ticks], xs.at[slot, 0])
-
-    def fetch_later():
-        for slot in (0, 1):
-            replica = parity if slot == 0 else 1 - parity
-            later = pl.ds(replica * ticks + 1, ticks - 1)
-            fetch(h_hbm.at[later], hs.at[slot, pl.ds(1, ticks - 1)])
-            fetch(x_hbm.at[later], xs.at[slot, pl.ds(1, ticks - 1)])
-        fetch(l_hbm.at[pl.ds((1 - parity) * (ticks - 1), ticks - 1)], loss)
+    for slot in (0, 1):
+        replica = parity if slot == 0 else 1 - parity
+        later = pl.ds(replica * ticks + 1, ticks - 1)
+        fetch(h_hbm.at[later], hs.at[slot, pl.ds(1, ticks - 1)])
+        fetch(x_hbm.at[later], xs.at[slot, pl.ds(1, ticks - 1)])
+    fetch(l_hbm.at[pl.ds((1 - parity) * (ticks - 1), ticks - 1)], loss)
 
     def wait(first, last):
         for copy in copies[first:last]:
             copy.wait()
 
-    fetch_first(0)
     wait(0, 3)
-    fetch_first(1)
-
-    def middle_of_slot_0():
-        wait(3, 5)
-        fetch_later()
-
     gx0[...] = step(
-        gs[0], xs.at[0, 0], hs.at[0, 0], ws.at[0], mg0, mh0, extent, middle_of_slot_0
+        gs[0], xs.at[0, 0], hs.at[0, 0], ws.at[0], mg0, mh0, extent, lambda: wait(3, 5)
     )
     wait(5, 8)
     gx1[...] = step(
@@ -179,9 +170,6 @@
         pltpu.make_async_copy(gx1_ref, edge_hbm.at[1 - parity], sems.at[1]),
     ]
     copies[0].start()
-    gx1_ref[...] = step(
-        g, x_ref.at[1, early], h_ref.at[1, early], w_ref.at[1], mg_ref, mh_ref, extent
-    )
     members, _, later, rows_each, _ = out_ref.shape
     upper = (position >= lax.axis_size("section") // 2).astype(jnp.int32)
     half0, half1 = (parity + upper) & 1, (1 - parity + upper) & 1
@@ -194,6 +182,9 @@
 
     for row in range(0, sums0_ref.shape[0], rows_each):
         put(row, half0, sums0_ref[row : row + rows_each, :])
+    gx1_ref[...] = step(
+        g, x_ref.at[1, early], h_ref.at[1, early], w_ref.at[1], mg_ref, mh_ref, extent
+    )
     copies[1].start()
     for pair, act_ref, moved_ref in ((0, x_ref, mh_ref), (1, h_ref, mg_ref)):
         total = kernel_sums([act_ref.at[1, early]], [moved_ref], extent)

time: 79 us -> 78.7 us (level)
  no operation moved by 1% of the time
where the time goes in v7:
time: 78.7 us; the launch traced here: 78.4 us
  blocking collectives  46.7 us (59%)
  starting transfers between devices  22.5 us (29%)
  Pallas kernels  6.63 us (8%)
  waiting for transfers between devices  1.05 us (1%)
  other arithmetic  0.81 us (1%)
    all_to_all x1, blocking collectives, whole(): lax.all_to_all(both, ('section', 'dp'), 0, 0, axis_index_groups=second_gr...  28.9 us
    ppermute x4, starting transfers between devices, exchange(): return lax.ppermute(value, 'section', pairs)  22.5 us
    all_to_all x1, blocking collectives, whole(): lax.all_to_all(both, 'dp', 0, 0, axis_index_groups=first_groups, tiled=True)  17.8 us
    pallas_call x6, Pallas kernels, call(): pl.pallas_call(body, in_specs=in_specs, out_specs=[in_hbm()] * hbm_outs +...  6.63 us
  transfers between devices with their start and end apart: 4, of which 2 were waited for; matrix products, arithmetic and copies ran while one was open for 0% of the time, Pallas kernels for 4%

profile of v7, /device:TPU:7, one launch (start us, length us, event | category | flops | bytes accessed | tf_op | source)
XLA Modules:
  0.0 78.4 jit_solution(6941821244640352123)
XLA Ops:
  0.6 2.5 %shard_map.68 = (bf16[2,3,256,128]{3,2,1,0:T(8,128)(2,1)S(1)}, bf16[2,3,256,128]{3,2,1,0:T(8,128)(2,1)S(1)}, bf16[2,2,9,128,128]{4,3,2,1,0:T(8,128)(2,1)S(1)}, b...) custom-call(bf16[6,256,128]{2,1,0:T(8,128)(2,1)} %bitcast.11, ...), custom_call_target="tpu_custom_call" | custom-call | flops 301989888 | bytes 1000000 | tf_op jit(solution)/shard_map/pallas_call | solution.py:199
  3.1 9.3 %collective-permute-start.2 = (bf16[256,128]{1,0:T(8,128)(2,1)S(1)}, bf16[256,128]{1,0:T(8,128)(2,1)S(1)}, u32[]{:S(2)}, u32[]{:S(2)}) collective-permute-start(bf16[256,128]{1,0:T(8,128)(2,1)S(1)} %get-tuple-element.30), channel_id=1, source_target_pairs={{16,32},{32,16},{48,64},{64,48},{80,96},{96,80},{112,128},{128,112... | collective-permute-start | bytes 196616 | tf_op jit(solution)/shard_map/ppermute | solution.py:227
  12.4 1.9 %collective-permute-start = (bf16[256,128]{1,0:T(8,128)(2,1)S(1)}, bf16[256,128]{1,0:T(8,128)(2,1)S(1)}, u32[]{:S(2)}, u32[]{:S(2)}) collective-permute-start(bf16[256,128]{1,0:T(8,128)(2,1)S(1)} %get-tuple-element.27), channel_id=1, source_target_pairs={{0,16},{16,0},{32,48},{48,32},{64,80},{80,64},{96,112},{112,96},{1... | collective-permute-start | bytes 196616 | tf_op jit(solution)/shard_map/ppermute | solution.py:227
  14.4 0.4 collective-permute-done.2.g_ref
  14.7 0.6 shard_map.70
  15.3 2.0 %collective-permute-start.3 = (bf16[256,128]{1,0:T(8,128)(2,1)S(1)}, bf16[256,128]{1,0:T(8,128)(2,1)S(1)}, u32[]{:S(2)}, u32[]{:S(2)}) collective-permute-start(bf16[256,128]{1,0:T(8,128)(2,1)S(1)} %get-tuple-element.31), channel_id=1, source_target_pairs={{0,16},{16,0},{32,48},{48,32},{64,80},{80,64},{96,112},{112,96},{1... | collective-permute-start | bytes 196616 | tf_op jit(solution)/shard_map/ppermute | solution.py:227
  17.4 0.0 collective-permute-done.g_ref
  17.4 0.6 shard_map.69
  17.9 9.2 %collective-permute-start.1 = (bf16[256,128]{1,0:T(8,128)(2,1)S(1)}, bf16[256,128]{1,0:T(8,128)(2,1)S(1)}, u32[]{:S(2)}, u32[]{:S(2)}) collective-permute-start(bf16[256,128]{1,0:T(8,128)(2,1)S(1)} %get-tuple-element.28), channel_id=1, source_target_pairs={{16,32},{32,16},{48,64},{64,48},{80,96},{96,80},{112,128},{128,112... | collective-permute-start | bytes 196616 | tf_op jit(solution)/shard_map/ppermute | solution.py:227
  27.1 1.0 %shard_map.71 = (f32[2304,128]{1,0:T(8,128)S(1)}, f32[2304,128]{1,0:T(8,128)S(1)}) custom-call(bf16[2,3,256,128]{3,2,1,0:T(8,128)(2,1)S(1)} %get-tuple-element.24.x_ref, bf16[2,3,256,128]{3,2,1,0:T(8,128)(2,1)S(1)} %get-tuple-element.25.h_ref, bf16[256,384]{1,0:T(8,128)(2,1)S(1)} %get-tuple-element.32.refs_0_, ...), custom_call_target="tpu_custom_call" | custom-call | flops 603979776 | bytes 1000000 | tf_op jit(solution)/shard_map/pallas_call | solution.py:199
  28.2 0.0 collective-permute-done.3.g_ref
  28.2 0.8 shard_map.72
  29.0 0.7 collective-permute-done.1.g_ref
  29.6 1.2 %shard_map.73 = (bf16[2,256,128]{2,1,0:T(8,128)(2,1)}, bf16[8,2,2,144,128]{4,3,2,1,0:T(8,128)(2,1)S(1)}) custom-call(bf16[2,3,256,128]{3,2,1,0:T(8,128)(2,1)S(1)} %get-tuple-element.24.x_ref, bf16[2,3,256,128]{3,2,1,0:T(8,128)(2,1)S(1)} %get-tuple-element.25.h_ref, bf16[2,2,9,128,128]{4,3,2,1,0:T(8,128)(2,1)S(1)} %get-tuple-element.26.w_ref, ...), custom_call_target="tpu_custom_call" | custom-call | flops 301989888 | bytes 1000000 | tf_op jit(solution)/shard_map/pallas_call | solution.py:199
  30.9 17.8 %all_to_all.10 = bf16[8,2,2,144,128]{4,3,2,1,0:T(8,128)(2,1)S(1)} all-to-all(bf16[8,2,2,144,128]{4,3,2,1,0:T(8,128)(2,1)S(1)} %get-tuple-element.44), channel_id=1, replica_groups={{0,1,4,5,8,9,12,13},{2,3,6,7,10,11,14,15},{16,17,20,21,24,25,28,29},{18..., dimensions={0} | all-to-all | bytes 2359296 | tf_op jit(solution)/shard_map/all_to_all | solution.py:350
  48.7 0.2 add_convert_fusion
  48.8 28.9 %all_to_all.11 = bf16[4,144,128]{2,1,0:T(8,128)(2,1)S(1)} all-to-all(bf16[4,144,128]{2,1,0:T(8,128)(2,1)S(1)} %bitcast.10), channel_id=1, replica_groups={{0,2,496,498},{1,3,497,499},{4,6,500,502},{5,7,501,503},{8,10,504,506},..., dimensions={0} | all-to-all | bytes 294912 | tf_op jit(solution)/shard_map/all_to_all | solution.py:352
  77.7 0.7 add_multiply_fusion
Async XLA Ops:
  3.1 11.6 %collective-permute-start.2 = (bf16[256,128]{1,0:T(8,128)(2,1)S(1)}, bf16[256,128]{1,0:T(8,128)(2,1)S(1)}, u32[]{:S(2)}, u32[]{:S(2)}) collective-permute-start(bf16[256,128]{1,0:T(8,128)(2,1)S(1)} %get-tuple-element.30), channel_id=1, source_target_pairs={{16,32},{32,16},{48,64},{64,48},{80,96},{96,80},{112,128},{128,112... | collective-permute-start | bytes 196616 | tf_op jit(solution)/shard_map/ppermute | solution.py:227
  12.4 4.9 %collective-permute-start = (bf16[256,128]{1,0:T(8,128)(2,1)S(1)}, bf16[256,128]{1,0:T(8,128)(2,1)S(1)}, u32[]{:S(2)}, u32[]{:S(2)}) collective-permute-start(bf16[256,128]{1,0:T(8,128)(2,1)S(1)} %get-tuple-element.27), channel_id=1, source_target_pairs={{0,16},{16,0},{32,48},{48,32},{64,80},{80,64},{96,112},{112,96},{1... | collective-permute-start | bytes 196616 | tf_op jit(solution)/shard_map/ppermute | solution.py:227
  15.3 12.9 %collective-permute-start.3 = (bf16[256,128]{1,0:T(8,128)(2,1)S(1)}, bf16[256,128]{1,0:T(8,128)(2,1)S(1)}, u32[]{:S(2)}, u32[]{:S(2)}) collective-permute-start(bf16[256,128]{1,0:T(8,128)(2,1)S(1)} %get-tuple-element.31), channel_id=1, source_target_pairs={{0,16},{16,0},{32,48},{48,32},{64,80},{80,64},{96,112},{112,96},{1... | collective-permute-start | bytes 196616 | tf_op jit(solution)/shard_map/ppermute | solution.py:227
  17.9 11.7 %collective-permute-start.1 = (bf16[256,128]{1,0:T(8,128)(2,1)S(1)}, bf16[256,128]{1,0:T(8,128)(2,1)S(1)}, u32[]{:S(2)}, u32[]{:S(2)}) collective-permute-start(bf16[256,128]{1,0:T(8,128)(2,1)S(1)} %get-tuple-element.28), channel_id=1, source_target_pairs={{16,32},{32,16},{48,64},{64,48},{80,96},{96,80},{112,128},{128,112... | collective-permute-start | bytes 196616 | tf_op jit(solution)/shard_map/ppermute | solution.py:227

commit v8 on v7

--- a/solution.py
+++ b/solution.py
@@ -161,15 +161,10 @@
 
 
 def last_kernel(extent, early, parts, x_ref, h_ref, w_ref, g_ref, loss_ref, *refs):
-    gx0_ref, sums0_ref, acc_ref, edge_hbm, out_ref, mg_ref, mh_ref, gx1_ref, sems = refs
+    sums0_ref, acc_ref, gx1_ref, out_ref, mg_ref, mh_ref = refs
     position = lax.axis_index("section")
     parity = position & 1
     g = (g_ref[...].astype(F32) + loss_ref[early - 1].astype(F32)).astype(BF16)
-    copies = [
-        pltpu.make_async_copy(gx0_ref, edge_hbm.at[parity], sems.at[0]),
-        pltpu.make_async_copy(gx1_ref, edge_hbm.at[1 - parity], sems.at[1]),
-    ]
-    copies[0].start()
     members, _, later, rows_each, _ = out_ref.shape
     upper = (position >= lax.axis_size("section") // 2).astype(jnp.int32)
     half0, half1 = (parity + upper) & 1, (1 - parity + upper) & 1
@@ -185,21 +180,28 @@
     gx1_ref[...] = step(
         g, x_ref.at[1, early], h_ref.at[1, early], w_ref.at[1], mg_ref, mh_ref, extent
     )
-    copies[1].start()
     for pair, act_ref, moved_ref in ((0, x_ref, mh_ref), (1, h_ref, mg_ref)):
         total = kernel_sums([act_ref.at[1, early]], [moved_ref], extent)
         for row, value in pieces(total, pair):
             put(row, half1, (value + acc_ref[row : row + PIECE, :]).astype(BF16))
-    for copy in copies:
-        copy.wait()
-
-
-def call(body, steps, in_specs, out_shape, scratch, args, hbm_outs=0):
+
+
+def finish_kernel(factor, parts_ref, gx0_ref, gx1_ref, sum_ref, edge_ref):
+    parity = lax.axis_index("section") & 1
+    edge_ref[parity] = gx0_ref[...]
+    edge_ref[1 - parity] = gx1_ref[...]
+    total = parts_ref[0].astype(F32)
+    for n in range(1, parts_ref.shape[0]):
+        total = total + parts_ref[n].astype(F32)
+    sum_ref[...] = total * factor
+
+
+def call(body, steps, in_specs, out_shape, scratch, args):
     cells, channels = args[0].shape[-2:]
     return pl.pallas_call(
         body,
         in_specs=in_specs,
-        out_specs=[in_hbm()] * hbm_outs + [vmem()] * (len(out_shape) - hbm_outs),
+        out_specs=[vmem()] * len(out_shape),
         out_shape=out_shape,
         scratch_shapes=scratch,
         compiler_params=PARAMS,
@@ -314,16 +316,14 @@
         scratch,
         (xs, hs, ws, near, acc0),
     )
-    edge, both = call(
+    out1, both = call(
         functools.partial(last_kernel, extent, early, outer),
         2,
-        [vmem()] * 8,
-        [shape(2), shape(2 * outer, 2, later, rows // shards, tail=(channels,))],
-        [*scratch, pltpu.VMEM(field, BF16), pltpu.SemaphoreType.DMA((2,))],
-        (xs, hs, ws, far, loss, out0, sums0, acc1),
-        hbm_outs=1,
-    )
-    edge_grads = edge.reshape(2, 1, 1, extent, extent, channels)
+        [vmem()] * 7,
+        [shape(), shape(2 * outer, 2, later, rows // shards, tail=(channels,))],
+        scratch,
+        (xs, hs, ws, far, loss, sums0, acc1),
+    )
 
     def shard(block, far, near):
         return (block * later + far) * 2 + near
@@ -352,8 +352,15 @@
     both = lax.all_to_all(
         both, ("section", "dp"), 0, 0, axis_index_groups=second_groups, tiled=True
     )
-    kernel_grads = (total(both) * (1.0 / float(cells)))[None]
-    return (kernel_grads, edge_grads)
+    kernel_grads, edge = call(
+        functools.partial(finish_kernel, 1.0 / float(cells)),
+        0,
+        [vmem()] * 3,
+        [jax.ShapeDtypeStruct((rows // shards, channels), F32), shape(2)],
+        [],
+        (both, out0, out1),
+    )
+    return (kernel_grads[None], edge.reshape(2, 1, 1, extent, extent, channels))
 
 
 def solution(mesh):

time: 78.7 us -> 78.3 us (level)
    pallas_call x6 -> x7, Pallas kernels: 6.63 us -> 6.88 us  [call(): pl.pallas_call(body, in_specs=in_specs, out_specs=[vmem()] * len(out_shap...]
where the time goes in v8:
time: 78.3 us; the launch traced here: 78 us
  blocking collectives  46.7 us (60%)
  starting transfers between devices  22.5 us (29%)
  Pallas kernels  6.88 us (9%)
  waiting for transfers between devices  1.05 us (1%)
    all_to_all x1, blocking collectives, whole(): lax.all_to_all(both, ('section', 'dp'), 0, 0, axis_index_groups=second_gr...  28.9 us
    ppermute x4, starting transfers between devices, exchange(): return lax.ppermute(value, 'section', pairs)  22.5 us
    all_to_all x1, blocking collectives, whole(): lax.all_to_all(both, 'dp', 0, 0, axis_index_groups=first_groups, tiled=True)  17.8 us
    pallas_call x7, Pallas kernels, call(): pl.pallas_call(body, in_specs=in_specs, out_specs=[vmem()] * len(out_shap...  6.88 us
  transfers between devices with their start and end apart: 4, of which 2 were waited for; matrix products, arithmetic and copies ran while one was open for 0% of the time, Pallas kernels for 4%

profile of v8, /device:TPU:7, one launch (start us, length us, event | category | flops | bytes accessed | tf_op | source)
XLA Modules:
  0.0 78.0 jit_solution(3223515008496007833)
XLA Ops:
  0.6 2.5 %shard_map.68 = (bf16[2,3,256,128]{3,2,1,0:T(8,128)(2,1)S(1)}, bf16[2,3,256,128]{3,2,1,0:T(8,128)(2,1)S(1)}, bf16[2,2,9,128,128]{4,3,2,1,0:T(8,128)(2,1)S(1)}, b...) custom-call(bf16[6,256,128]{2,1,0:T(8,128)(2,1)} %bitcast.12, ...), custom_call_target="tpu_custom_call" | custom-call | flops 301989888 | bytes 1000000 | tf_op jit(solution)/shard_map/pallas_call | solution.py:201
  3.1 9.3 %collective-permute-start.2 = (bf16[256,128]{1,0:T(8,128)(2,1)S(1)}, bf16[256,128]{1,0:T(8,128)(2,1)S(1)}, u32[]{:S(2)}, u32[]{:S(2)}) collective-permute-start(bf16[256,128]{1,0:T(8,128)(2,1)S(1)} %get-tuple-element.32), channel_id=1, source_target_pairs={{16,32},{32,16},{48,64},{64,48},{80,96},{96,80},{112,128},{128,112... | collective-permute-start | bytes 196616 | tf_op jit(solution)/shard_map/ppermute | solution.py:229
  12.4 1.9 %collective-permute-start = (bf16[256,128]{1,0:T(8,128)(2,1)S(1)}, bf16[256,128]{1,0:T(8,128)(2,1)S(1)}, u32[]{:S(2)}, u32[]{:S(2)}) collective-permute-start(bf16[256,128]{1,0:T(8,128)(2,1)S(1)} %get-tuple-element.29), channel_id=1, source_target_pairs={{0,16},{16,0},{32,48},{48,32},{64,80},{80,64},{96,112},{112,96},{1... | collective-permute-start | bytes 196616 | tf_op jit(solution)/shard_map/ppermute | solution.py:229
  14.4 0.4 collective-permute-done.2.g_ref
  14.7 0.6 shard_map.70
  15.3 2.0 %collective-permute-start.3 = (bf16[256,128]{1,0:T(8,128)(2,1)S(1)}, bf16[256,128]{1,0:T(8,128)(2,1)S(1)}, u32[]{:S(2)}, u32[]{:S(2)}) collective-permute-start(bf16[256,128]{1,0:T(8,128)(2,1)S(1)} %get-tuple-element.33), channel_id=1, source_target_pairs={{0,16},{16,0},{32,48},{48,32},{64,80},{80,64},{96,112},{112,96},{1... | collective-permute-start | bytes 196616 | tf_op jit(solution)/shard_map/ppermute | solution.py:229
  17.4 0.0 collective-permute-done.g_ref
  17.4 0.6 shard_map.69
  17.9 9.2 %collective-permute-start.1 = (bf16[256,128]{1,0:T(8,128)(2,1)S(1)}, bf16[256,128]{1,0:T(8,128)(2,1)S(1)}, u32[]{:S(2)}, u32[]{:S(2)}) collective-permute-start(bf16[256,128]{1,0:T(8,128)(2,1)S(1)} %get-tuple-element.30), channel_id=1, source_target_pairs={{16,32},{32,16},{48,64},{64,48},{80,96},{96,80},{112,128},{128,112... | collective-permute-start | bytes 196616 | tf_op jit(solution)/shard_map/ppermute | solution.py:229
  27.1 1.0 %shard_map.71 = (f32[2304,128]{1,0:T(8,128)S(1)}, f32[2304,128]{1,0:T(8,128)S(1)}) custom-call(bf16[2,3,256,128]{3,2,1,0:T(8,128)(2,1)S(1)} %get-tuple-element.26.x_ref, bf16[2,3,256,128]{3,2,1,0:T(8,128)(2,1)S(1)} %get-tuple-element.27.h_ref, bf16[256,384]{1,0:T(8,128)(2,1)S(1)} %get-tuple-element.34.refs_0_, ...), custom_call_target="tpu_custom_call" | custom-call | flops 603979776 | bytes 1000000 | tf_op jit(solution)/shard_map/pallas_call | solution.py:201
  28.2 0.0 collective-permute-done.3.g_ref
  28.2 0.8 %shard_map.72 = (bf16[256,128]{1,0:T(8,128)(2,1)S(1)}, bf16[2304,128]{1,0:T(8,128)(2,1)S(1)}) custom-call(bf16[2,3,256,128]{3,2,1,0:T(8,128)(2,1)S(1)} %get-tuple-element.26.x_ref, bf16[2,3,256,128]{3,2,1,0:T(8,128)(2,1)S(1)} %get-tuple-element.27.h_ref, bf16[2,2,9,128,128]{4,3,2,1,0:T(8,128)(2,1)S(1)} %get-tuple-element.28.w_ref, ...), custom_call_target="tpu_custom_call" | custom-call | flops 301989888 | bytes 1000000 | tf_op jit(solution)/shard_map/pallas_call | solution.py:201
  29.0 0.7 collective-permute-done.1.g_ref
  29.6 0.8 shard_map.73
  30.4 17.8 %all_to_all.10 = bf16[8,2,2,144,128]{4,3,2,1,0:T(8,128)(2,1)S(1)} all-to-all(bf16[8,2,2,144,128]{4,3,2,1,0:T(8,128)(2,1)S(1)} %get-tuple-element.45), channel_id=1, replica_groups={{0,1,4,5,8,9,12,13},{2,3,6,7,10,11,14,15},{16,17,20,21,24,25,28,29},{18..., dimensions={0} | all-to-all | bytes 2359296 | tf_op jit(solution)/shard_map/all_to_all | solution.py:350
  48.2 0.2 add_convert_fusion
  48.4 28.9 %all_to_all.11.parts_ref = bf16[4,144,128]{2,1,0:T(8,128)(2,1)S(1)} all-to-all(bf16[4,144,128]{2,1,0:T(8,128)(2,1)S(1)} %bitcast.11), channel_id=1, replica_groups={{0,2,496,498},{1,3,497,499},{4,6,500,502},{5,7,501,503},{8,10,504,506},..., dimensions={0} | all-to-all | bytes 294912 | tf_op jit(solution)/shard_map/all_to_all | solution.py:352
  77.3 0.7 shard_map.74
Async XLA Ops:
  3.1 11.6 %collective-permute-start.2 = (bf16[256,128]{1,0:T(8,128)(2,1)S(1)}, bf16[256,128]{1,0:T(8,128)(2,1)S(1)}, u32[]{:S(2)}, u32[]{:S(2)}) collective-permute-start(bf16[256,128]{1,0:T(8,128)(2,1)S(1)} %get-tuple-element.32), channel_id=1, source_target_pairs={{16,32},{32,16},{48,64},{64,48},{80,96},{96,80},{112,128},{128,112... | collective-permute-start | bytes 196616 | tf_op jit(solution)/shard_map/ppermute | solution.py:229
  12.4 4.9 %collective-permute-start = (bf16[256,128]{1,0:T(8,128)(2,1)S(1)}, bf16[256,128]{1,0:T(8,128)(2,1)S(1)}, u32[]{:S(2)}, u32[]{:S(2)}) collective-permute-start(bf16[256,128]{1,0:T(8,128)(2,1)S(1)} %get-tuple-element.29), channel_id=1, source_target_pairs={{0,16},{16,0},{32,48},{48,32},{64,80},{80,64},{96,112},{112,96},{1... | collective-permute-start | bytes 196616 | tf_op jit(solution)/shard_map/ppermute | solution.py:229
  15.3 12.9 %collective-permute-start.3 = (bf16[256,128]{1,0:T(8,128)(2,1)S(1)}, bf16[256,128]{1,0:T(8,128)(2,1)S(1)}, u32[]{:S(2)}, u32[]{:S(2)}) collective-permute-start(bf16[256,128]{1,0:T(8,128)(2,1)S(1)} %get-tuple-element.33), channel_id=1, source_target_pairs={{0,16},{16,0},{32,48},{48,32},{64,80},{80,64},{96,112},{112,96},{1... | collective-permute-start | bytes 196616 | tf_op jit(solution)/shard_map/ppermute | solution.py:229
  17.9 11.7 %collective-permute-start.1 = (bf16[256,128]{1,0:T(8,128)(2,1)S(1)}, bf16[256,128]{1,0:T(8,128)(2,1)S(1)}, u32[]{:S(2)}, u32[]{:S(2)}) collective-permute-start(bf16[256,128]{1,0:T(8,128)(2,1)S(1)} %get-tuple-element.30), channel_id=1, source_target_pairs={{16,32},{32,16},{48,64},{64,48},{80,96},{96,80},{112,128},{128,112... | collective-permute-start | bytes 196616 | tf_op jit(solution)/shard_map/ppermute | solution.py:229
